TPU v7x, 512 devices: a whole 4x8x8 slice. The times are simulated.
512 devices in a mesh: dp: 16 (over z, core), ctx: 32 (over x, y).
Axes of the slice: x: 4, y: 8, z: 8, core: 2. Of those that a mesh axis runs over, the one named last changes fastest.
Arguments:
- streams: bfloat16 [3, 1, 10240, 8192], P(None, None, 'ctx', 'dp'), may hold values from -6 to 6
- cotangent: bfloat16 [1, 10240, 8192], P(None, 'ctx', 'dp'), may hold values from -6 to 6
- counts: int32 [1, 32], P(None, 'ctx'), may hold values from 1 to 320, as said below
- short_filters: bfloat16 [3, 7, 8192], P(None, None, ('dp', 'ctx')), may hold values from -14 to 14
- long_filter: bfloat16 [128, 8192], P(None, ('dp', 'ctx')), may hold values from -0.5 to 0.5
Outputs:
- stream_grads: bfloat16 [3, 1, 10240, 8192], P(None, None, 'ctx', 'dp')
- long_grad: float32 [128, 8192], P(None, ('dp', 'ctx'))
- short_grad: float32 [3, 7, 8192], P(None, None, ('dp', 'ctx'))
Inputs may be any that keep to these rules, and one draw needn't show every extreme that they name: In each window the counts sum to 8192, and one of them equals 320.
All inputs are finite; a program needn't handle non-finite values.
Results may differ from a plain program's by a relative error of at most 0.0058.
Values may be sent and summed in bfloat16 or wider, within the bound.
No kernel may reach another device: no remote copies, remote signals or barrier semaphores. Data moves between devices by JAX's collectives and lax.ppermute only.
A program may use at most 64 MiB of HBM per device.

v0:
```python
import functools

import jax
import jax.numpy as jnp
from jax import lax
from jax.sharding import Mesh
from jax.sharding import PartitionSpec as P

CH = 8192
LTAP = 128
STAP = 7
CTX = ("ctx_0", "ctx_1")
DP_CTX = ("dp_0", "dp_1", "ctx_0", "ctx_1")
DP = ("dp_0", "dp_1")


def rows_first(arrays, axis, dims):
    turned = [jnp.moveaxis(a, dim, 0) for a, dim in zip(arrays, dims)]
    widths = [t[0].size for t in turned]
    both = jnp.concatenate([t.reshape(-1, w) for t, w in zip(turned, widths)], axis=1)
    result = lax.all_gather(both, axis, axis=0, tiled=True)
    blocks = jnp.split(result, [sum(widths[:k]) for k in range(1, len(widths))], axis=1)
    return tuple(
        (
            jnp.moveaxis(b.reshape(-1, *t.shape[1:]), 0, dim)
            for b, t, dim in zip(blocks, turned, dims)
        )
    )


def from_everyone(shard, axis):
    count = lax.axis_size(axis)
    return lax.all_to_all(
        jnp.broadcast_to(shard[None], (count, *shard.shape)), axis, 0, 0, tiled=True
    )


def collected_together(shard, axis):
    leaves = jax.tree.leaves(shard)
    turns = sorted(range(len(leaves)), key=lambda k: -leaves[k].size)
    width = (1, *leaves[turns[0]].shape)[-1]
    lines = [
        jnp.pad(leaves[k].reshape(-1), (0, -leaves[k].size % width)).reshape(-1, width)
        for k in turns
    ]
    both, at, found = (from_everyone(jnp.concatenate(lines), axis), 0, {})
    for k, line in zip(turns, lines):
        share = both[:, at : at + len(line)].reshape(len(both), -1)
        found[k] = share[:, : leaves[k].size].reshape(-1, *leaves[k].shape)
        at += len(line)
    numbers = iter(range(len(leaves)))
    return jax.tree.map(lambda _: found[next(numbers)], shard)


def folded_in_pairs(pieces, combine):
    while len(jax.tree.leaves(pieces)[0]) > 1:
        pieces = jax.vmap(combine)(
            *(jax.tree.map(lambda part: part[side::2], pieces) for side in (0, 1))
        )
    return jax.tree.map(lambda part: part[0], pieces)


def carried_in(shard, axis, combine, identity, reverse):
    count, here = (lax.axis_size(axis), lax.axis_index(axis))
    passed = jnp.arange(count) > here if reverse else jnp.arange(count) < here

    def kept(part, zero, own):
        part = jnp.where(
            passed.reshape(-1, *(1 for _ in own.shape)), part, jnp.asarray(zero, own.dtype)
        )
        return part[::-1] if reverse else part

    pieces = collected_together(shard, axis)
    return folded_in_pairs(jax.tree.map(kept, pieces, identity, shard), combine)


def neutral_like(shard, identity):
    return jax.tree.map(
        lambda part, zero: jnp.zeros_like(part) + jnp.asarray(zero, part.dtype), shard, identity
    )


def entering(shard, axes, combine, identity, reverse):
    before = start = neutral_like(shard, identity)
    running = shard
    for axis in reversed(axes):
        count, here = (lax.axis_size(axis), lax.axis_index(axis))
        pieces = jax.tree.map(lambda part: lax.all_gather(part, axis), running)
        inside, running = (start, start)
        for k in reversed(range(count)) if reverse else range(count):
            passed = k > here if reverse else k < here
            running = combine(running, jax.tree.map(lambda part: part[k], pieces))
            inside = jax.tree.map(lambda new, old: jnp.where(passed, new, old), running, inside)
        before = combine(inside, before)
    return before


def split_up(shard, dim, count):
    shape = shard.shape
    blocks = shard.reshape(*shape[:dim], count, shape[dim] // count, *shape[dim + 1 :])
    return jnp.moveaxis(blocks, dim, 0)


def sum_at_owner(shard, axis, dim):
    count = lax.axis_size(axis)
    blocks = lax.all_to_all(split_up(shard, dim, count), axis, 0, 0, tiled=True)
    return jnp.sum(blocks, axis=0)


def over_axes(shard, axes):
    return functools.reduce(lax.psum, axes, shard)


def causal_long(lead, filt, length):
    reach = filt.shape[0] - 1

    def causal_add_tap(tap_index, total):
        piece = lax.dynamic_slice_in_dim(lead, reach - tap_index, length, 0)
        return total + filt[tap_index].astype(jnp.float32)[None, :] * piece.astype(jnp.float32)

    return lax.fori_loop(
        0, filt.shape[0], causal_add_tap, jnp.zeros((length, filt.shape[1]), jnp.float32)
    )


def anticausal_long(trail, filt, length):

    def anticausal_add_tap(tap_index, total):
        piece = lax.dynamic_slice_in_dim(trail, tap_index, length, 0)
        return total + filt[tap_index].astype(jnp.float32)[None, :] * piece.astype(jnp.float32)

    return lax.fori_loop(
        0, filt.shape[0], anticausal_add_tap, jnp.zeros((length, filt.shape[1]), jnp.float32)
    )


def tap_products(lead, grad_rows, taps):
    reach = taps - 1
    length = grad_rows.shape[0]

    def one_tap(tap_index):
        piece = lax.dynamic_slice_in_dim(lead, reach - tap_index, length, 0)
        return jnp.sum(grad_rows.astype(jnp.float32) * piece.astype(jnp.float32), axis=0)

    return lax.map(one_tap, jnp.arange(taps, dtype=jnp.int32))


def short_forward(leading, filters, length):
    taps = filters.shape[1]
    summed = jnp.zeros((filters.shape[0], length, filters.shape[2]), jnp.float32)
    for tap_index in range(taps):
        start = taps - 1 - tap_index
        summed = summed + filters[:, tap_index][:, None, :].astype(jnp.float32) * leading[
            :, start : start + length
        ].astype(jnp.float32)
    return summed


def short_backward(trailing, filters, length):
    taps = filters.shape[1]
    summed = jnp.zeros((filters.shape[0], length, filters.shape[2]), jnp.float32)
    for tap_index in range(taps):
        summed = summed + filters[:, tap_index][:, None, :].astype(jnp.float32) * trailing[
            :, tap_index : tap_index + length
        ].astype(jnp.float32)
    return summed


def last_rows(block, live_count, length):
    zero_rows = jnp.zeros(block.shape[:-2] + (length, block.shape[-1]), block.dtype)
    padded = jnp.concatenate([zero_rows, block], axis=-2)
    return lax.dynamic_slice_in_dim(padded, live_count, length, axis=block.ndim - 2)


def first_rows(block, length):
    zero_rows = jnp.zeros(block.shape[:-2] + (length, block.shape[-1]), block.dtype)
    padded = jnp.concatenate([block, zero_rows], axis=-2)
    return padded[..., :length, :]


def fill_of(live_count, length):
    return jnp.minimum(live_count, length).astype(jnp.bfloat16).reshape(1)


def join_fills(earlier, later):
    longest = max((member.shape[-2] for member in earlier[:-1]))
    summed = earlier[-1].astype(jnp.float32) + later[-1].astype(jnp.float32)
    return jnp.minimum(summed, float(longest)).astype(earlier[-1].dtype)


def join_tails(earlier, later):
    moved_by = later[-1][0].astype(jnp.int32)
    joined = []
    for before, after in zip(earlier[:-1], later[:-1]):
        length = before.shape[-2]
        extended = jnp.concatenate([before, jnp.zeros_like(before)], axis=-2)
        moved = lax.dynamic_slice_in_dim(extended, moved_by, length, axis=before.ndim - 2)
        row_ids = lax.broadcasted_iota(jnp.int32, (length, 1), 0)
        joined.append(jnp.where(row_ids >= length - moved_by, after, moved))
    return tuple(joined) + (join_fills(earlier, later),)


def join_heads(earlier, later):
    moved_by = later[-1][0].astype(jnp.int32)
    joined = []
    for further, nearer in zip(earlier[:-1], later[:-1]):
        length = further.shape[-2]
        extended = jnp.concatenate([jnp.zeros_like(further), further], axis=-2)
        moved = lax.dynamic_slice_in_dim(extended, length - moved_by, length, axis=further.ndim - 2)
        row_ids = lax.broadcasted_iota(jnp.int32, (length, 1), 0)
        joined.append(jnp.where(row_ids < moved_by, nearer, moved))
    return tuple(joined) + (join_fills(earlier, later),)


def local(streams, cotangent, counts, short_filters, long_filter):
    live_count = counts[0, 0]
    slot_count = streams.shape[2]
    channels = streams.shape[3]
    reach = LTAP - 1
    short_reach = STAP - 1
    zero_fill = jnp.zeros((1,), jnp.bfloat16)
    live = lax.broadcasted_iota(jnp.int32, (slot_count, 1), 0) < live_count
    source = jnp.where(live[None], streams[:, 0], jnp.zeros((), streams.dtype))
    grad_out = jnp.where(live, cotangent[0], jnp.zeros((), cotangent.dtype))
    long_full, short_full = rows_first((long_filter, short_filters), CTX, (1, 2))
    short_tail = last_rows(source, live_count, short_reach)
    short_halo, _ = carried_in(
        (short_tail, fill_of(live_count, short_reach)),
        CTX,
        join_tails,
        (jnp.zeros_like(short_tail), zero_fill),
        False,
    )
    leading = jnp.concatenate([short_halo, source], axis=1)
    feats = short_forward(leading, short_full, slot_count)
    query, keys, values = (feats[0], feats[1], feats[2])
    gated = jnp.where(live, keys * values, 0.0).astype(jnp.bfloat16)
    gated_tail = last_rows(gated, live_count, reach)
    gated_halo, _ = entering(
        (gated_tail, fill_of(live_count, reach)),
        CTX,
        join_tails,
        (jnp.zeros_like(gated_tail), zero_fill),
        False,
    )
    gated_lead = jnp.concatenate([gated_halo, gated], axis=0)
    long_out = causal_long(gated_lead, long_full, slot_count)
    grad_query = (grad_out * long_out).astype(jnp.bfloat16)
    grad_long = (grad_out * query).astype(jnp.bfloat16)
    long_head = first_rows(grad_long, reach)
    long_halo, _ = entering(
        (long_head, fill_of(live_count, reach)),
        CTX,
        join_heads,
        (jnp.zeros_like(long_head), zero_fill),
        True,
    )
    trailing = jnp.concatenate([grad_long, jnp.zeros((reach, channels), jnp.bfloat16)], axis=0)
    trailing = lax.dynamic_update_slice_in_dim(trailing, long_halo, live_count, 0)
    grad_gated = anticausal_long(trailing, long_full, slot_count)
    grad_keys = jnp.where(live, grad_gated * values, 0.0).astype(jnp.bfloat16)
    grad_values = jnp.where(live, grad_gated * keys, 0.0).astype(jnp.bfloat16)
    grads = jnp.stack([grad_query, grad_keys, grad_values])
    grad_head = first_rows(grads, short_reach)
    grad_halo, _ = carried_in(
        (grad_head, fill_of(live_count, short_reach)),
        CTX,
        join_heads,
        (jnp.zeros_like(grad_head), zero_fill),
        True,
    )
    grad_trail = jnp.concatenate(
        [grads, jnp.zeros((3, short_reach, channels), jnp.bfloat16)], axis=1
    )
    grad_trail = lax.dynamic_update_slice_in_dim(grad_trail, grad_halo, live_count, 1)
    back = short_backward(grad_trail, short_full, slot_count)
    stream_grads = jnp.where(live[None], back, 0.0).astype(jnp.bfloat16)[:, None]
    long_term = tap_products(gated_lead, grad_long, LTAP)
    short_terms = []
    for tap_index in range(STAP):
        start = short_reach - tap_index
        short_terms.append(
            jnp.sum(
                grads.astype(jnp.float32)
                * leading[:, start : start + slot_count].astype(jnp.float32),
                axis=1,
            )
        )
    short_term = jnp.stack(short_terms, axis=1)
    grad_rows = jnp.concatenate([long_term, short_term.reshape(3 * STAP, channels)], axis=0)
    own_share = sum_at_owner(grad_rows, CTX, 1)
    squares = over_axes(jnp.sum(own_share * own_share), DP_CTX)
    rms = jnp.sqrt(squares / float((LTAP + 3 * STAP) * CH) + 1e-06)
    normed = own_share / rms
    long_grad = normed[:LTAP]
    short_grad = normed[LTAP:].reshape(3, STAP, normed.shape[1])
    return (stream_grads, long_grad, short_grad)


def solution(mesh):
    finer = Mesh(mesh.devices.reshape(8, 2, 4, 8), ("dp_0", "dp_1", "ctx_0", "ctx_1"))
    return jax.shard_map(
        local,
        mesh=finer,
        in_specs=(
            P(None, None, CTX, DP),
            P(None, CTX, DP),
            P(None, CTX),
            P(None, None, DP_CTX),
            P(None, DP_CTX),
        ),
        out_specs=(P(None, None, CTX, DP), P(None, DP_CTX), P(None, None, DP_CTX)),
        check_vma=False,
    )
```

profile of v0, /device:TPU:8, one launch (start us, length us, event | category | flops | bytes accessed | tf_op | source)
XLA Modules:
  0.0 889.6 jit_solution(13611029997971728119)
XLA Ops:
  1.3 1.3 bitcast_select_fusion
  2.8 0.9 broadcast_in_dim.343
  3.7 10.2 %all-to-all-start = ((bf16[32,19,512]{2,1,0:T(8,128)(2,1)}), bf16[32,19,512]{2,1,0:T(8,128)(2,1)S(1)}, u32[]{:S(2)}, u32[]{:S(2)}) async-start(bf16[32,19,512]{2,1,0:T(8,128)(2,1)} %broadcast_in_dim.343), calls=%async_computation | async-start | bytes 1572864 | tf_op jit(solution)/shard_map/all_to_all | solution.py:33
  13.9 1.3 dynamic-slice.8
  15.2 0.8 dynamic-update-slice.2
  16.0 25.4 %all-reduce.37 = bf16[8]{0:T(256)(128)(2,1)S(1)} all-reduce(bf16[8]{0:T(256)(128)(2,1)S(1)} %dynamic-update-slice.2), channel_id=1, replica_groups=mesh['dp_0'=8,'dp_1'=2,'ctx_0'=4,'ctx_1'=8] {'ctx_1'}, use_global_device_ids=true, to_apply=%add.37 | all-reduce | flops 8 | bytes 32
  42.6 1.2 fusion.115
  43.9 1.2 fusion.114
  45.1 1.9 fusion.113
  51.5 1.3 dynamic-slice.9
  52.8 1.8 fusion.105
  54.6 2.0 fusion.96
  56.6 1.8 minimum_convert_fusion.11
  58.4 1.9 minimum_convert_fusion.10
  60.4 1.3 dynamic-update-slice.3
  61.7 1.2 dynamic-update-slice.4
  63.0 10.5 %all-reduce.40 = (bf16[4]{0:T(256)(128)(2,1)S(1)}, bf16[4]{0:T(256)(128)(2,1)S(1)}) all-reduce(bf16[4]{0:T(256)(128)(2,1)S(1)} %dynamic-update-slice.4, bf16[4]{0:T(256)(128)(2,1)S(1)} %dynamic-update-slice.3), channel_id=6, replica_groups=mesh['dp_0'=8,'dp_1'=2,'ctx_0'=4,'ctx_1'=8] {'ctx_0'}, use_global_device_ids=true, to_apply=%add.39 | all-reduce | flops 8 | bytes 32
  81.8 49.4 %all_gather.43 = bf16[512,149]{1,0:T(8,128)(2,1)S(1)} all-gather(bf16[16,149]{1,0:T(8,128)(2,1)S(1)} %pad_maximum_fusion.5), channel_id=1, replica_groups=mesh['dp_0'=8,'dp_1'=2,'ctx_0'=4,'ctx_1'=8] {'ctx_0','ctx_1'}, dimensions={0}, use_global_device_ids=true | all-gather | bytes 157344 | tf_op jit(solution)/shard_map/all_gather | solution.py:21
  151.1 0.8 copy.94
  155.7 0.7 fusion.68
  159.3 1.1 concatenate.164.clone
  160.4 2.1 gather_fusion
  162.9 0.7 copy-done.5
  164.0 0.7 gather_fusion.1
  164.7 1.2 slice_select_fusion.2
  169.4 1.8 fusion.5
  171.7 26.1 %all-gather.6 = bf16[8,127,512]{2,1,0:T(8,128)(2,1)S(1)} all-gather(bf16[1,127,512]{2,1,0:T(8,128)(2,1)S(1)} %fusion.48), channel_id=2, replica_groups=mesh['dp_0'=8,'dp_1'=2,'ctx_0'=4,'ctx_1'=8] {'ctx_1'}, dimensions={0}, use_global_device_ids=true | all-gather | bytes 1170432 | tf_op jit(solution)/shard_map/all_gather | solution.py:88
  198.8 12.8 %all-gather.7 = bf16[4,127,512]{2,1,0:T(8,128)(2,1)S(1)} all-gather(bf16[1,127,512]{2,1,0:T(8,128)(2,1)S(1)} %fusion.109), channel_id=4, replica_groups=mesh['dp_0'=8,'dp_1'=2,'ctx_0'=4,'ctx_1'=8] {'ctx_0'}, dimensions={0}, use_global_device_ids=true | all-gather | bytes 650240 | tf_op jit(solution)/shard_map/all_gather | solution.py:88
  212.6 130.4 %while.45 = (s32[]{:T(128)}, f32[320,512]{1,0:T(8,128)S(1)}, bf16[128,512]{1,0:T(8,128)(2,1)}, bf16[447,512]{1,0:T(8,128)(2,1)S(1)}, s32[]{:T(128)}, /*index=5*/s32[]{:T(128)}, s32[]{:T(128)}, s32[]{:T(128)}) while((s32[]{:T(128)}, f32[320,512]{1,0:T(8,128)S(1)}, bf16[128,512]{1,0:T(8,128)(2,1)}, bf16[447,512]{1,0:T(8,128)(2,1)S(1)}, ...), condition=%wide.region_1.2_spmd.clone, body=%wide.region_0.1_spmd.clone.sunk | while | flops 655879 | bytes 1643669 | solution.py:121
  212.7 0.7 dynamic-slice_convert_fusion.4
  213.7 0.7 dynamic-slice_convert_fusion.4
  214.7 0.7 dynamic-slice_convert_fusion.4
  219.8 0.7 dynamic-slice_convert_fusion.4
  220.8 0.7 dynamic-slice_convert_fusion.4
  221.8 0.7 dynamic-slice_convert_fusion.4
  222.8 0.7 dynamic-slice_convert_fusion.4
  223.9 0.7 dynamic-slice_convert_fusion.4
  224.9 0.7 dynamic-slice_convert_fusion.4
  225.9 0.7 dynamic-slice_convert_fusion.4
  226.9 0.7 dynamic-slice_convert_fusion.4
  227.9 0.7 dynamic-slice_convert_fusion.4
  228.9 0.7 dynamic-slice_convert_fusion.4
  230.0 0.7 dynamic-slice_convert_fusion.4
  231.0 0.7 dynamic-slice_convert_fusion.4
  343.1 26.3 %all-gather.8 = bf16[8,127,512]{2,1,0:T(8,128)(2,1)S(1)} all-gather(bf16[1,127,512]{2,1,0:T(8,128)(2,1)S(1)} %slice_bitcast_fusion.15), channel_id=5, replica_groups=mesh['dp_0'=8,'dp_1'=2,'ctx_0'=4,'ctx_1'=8] {'ctx_1'}, dimensions={0}, use_global_device_ids=true | all-gather | bytes 1170432 | tf_op jit(solution)/shard_map/all_gather | solution.py:88
  370.4 12.8 %all-gather.9 = bf16[4,127,512]{2,1,0:T(8,128)(2,1)S(1)} all-gather(bf16[1,127,512]{2,1,0:T(8,128)(2,1)S(1)} %fusion.108), channel_id=7, replica_groups=mesh['dp_0'=8,'dp_1'=2,'ctx_0'=4,'ctx_1'=8] {'ctx_0'}, dimensions={0}, use_global_device_ids=true | all-gather | bytes 650240 | tf_op jit(solution)/shard_map/all_gather | solution.py:88
  383.9 1.0 fusion.47
  384.9 1.6 dynamic_update_slice.13
  386.6 129.7 %while.46 = (s32[]{:T(128)}, f32[320,512]{1,0:T(8,128)S(1)}, bf16[128,512]{1,0:T(8,128)(2,1)}, bf16[447,512]{1,0:T(8,128)(2,1)S(1)}, s32[]{:T(128)}, /*index=5*/s32[]{:T(128)}) while((s32[]{:T(128)}, f32[320,512]{1,0:T(8,128)S(1)}, bf16[128,512]{1,0:T(8,128)(2,1)}, bf16[447,512]{1,0:T(8,128)(2,1)S(1)}, s32[]{:T(128)}, ...), condition=%wide.region_3.4_spmd.clone, body=%wide.region_2.3_spmd.clone.sunk | while | flops 655875 | bytes 1643607 | solution.py:132
  516.3 1.6 fusion.21
  517.9 2.0 fusion.11
  520.6 272.5 %while.44 = (s32[]{:T(128)}, f32[128,512]{1,0:T(8,128)S(1)}, bf16[320,512]{1,0:T(8,128)(2,1)S(1)}, s32[128]{0:T(128)S(1)}, bf16[447,512]{1,0:T(8,128)(2,1)S(1)},...) while((s32[]{:T(128)}, f32[128,512]{1,0:T(8,128)S(1)}, bf16[320,512]{1,0:T(8,128)(2,1)S(1)}, ...), condition=%wide.region_6.7_spmd, body=%wide.region_4.6_spmd.sunk | while | flops 654854 | bytes 661663 | solution.py:145
  793.3 0.8 maximum_bitcast_fusion
  794.1 7.6 all-to-all-start.2
  801.9 13.2 %all-to-all-done.2 = f32[32,149,16]{1,2,0:T(8,128)S(1)} async-done(((f32[32,149,16]{1,2,0:T(8,128)}), f32[32,149,16]{1,2,0:T(8,128)S(1)}, u32[]{:S(2)}, u32[]{:S(2)}) %all-to-all-start.2) | async-done | bytes 305184 | tf_op jit(solution)/shard_map/all_to_all | solution.py:106
  815.2 0.9 broadcast_in_dim.377
  816.1 4.8 all-to-all-start.1
  821.6 23.8 %psum.28 = f32[]{:T(128)} all-reduce(f32[]{:T(128)} %multiply_reduce_fusion.1), channel_id=1, replica_groups=mesh['dp_0'=8,'dp_1'=2,'ctx_0'=4,'ctx_1'=8] {'dp_0'}, use_global_device_ids=true, to_apply=%region_16.17 | all-reduce | flops 1 | bytes 8 | tf_op jit(solution)/shard_map/psum | solution.py:111
  845.4 3.1 psum.29
  848.5 11.1 %psum.30 = f32[]{:T(128)} all-reduce(f32[]{:T(128)} %psum.29), channel_id=1, replica_groups=mesh['dp_0'=8,'dp_1'=2,'ctx_0'=4,'ctx_1'=8] {'ctx_0'}, use_global_device_ids=true, to_apply=%region_18.19 | all-reduce | flops 1 | bytes 8 | tf_op jit(solution)/shard_map/psum | solution.py:111
  859.6 16.3 %psum.31 = f32[]{:T(128)} all-reduce(f32[]{:T(128)} %psum.30), channel_id=1, replica_groups=mesh['dp_0'=8,'dp_1'=2,'ctx_0'=4,'ctx_1'=8] {'ctx_1'}, use_global_device_ids=true, to_apply=%region_19.20 | all-reduce | flops 1 | bytes 8 | tf_op jit(solution)/shard_map/psum | solution.py:111
  880.4 0.9 gather_fusion.4
  882.2 0.7 gather_fusion.5
  886.8 2.7 fusion.18
  (1205 shorter events, 383.5 us)
Async XLA Ops:
  1.3 1.4 copy-start.22
  2.6 79.1 %copy-start.25 = (bf16[3,7,16]{2,1,0:T(8,128)(2,1)S(1)}, bf16[3,7,16]{2,1,0:T(8,128)(2,1)}, u32[]{:S(2)}) copy-start(bf16[3,7,16]{2,1,0:T(8,128)(2,1)} %param.14) | copy-start | bytes 2020
  2.7 79.2 %copy-start.26 = (bf16[128,16]{0,1:T(8,128)(2,1)S(1)}, bf16[128,16]{0,1:T(8,128)(2,1)}, u32[]{:S(2)}) copy-start(bf16[128,16]{0,1:T(8,128)(2,1)} %param.15) | copy-start | bytes 12292
  3.7 151.6 %all-to-all-start = ((bf16[32,19,512]{2,1,0:T(8,128)(2,1)}), bf16[32,19,512]{2,1,0:T(8,128)(2,1)S(1)}, u32[]{:S(2)}, u32[]{:S(2)}) async-start(bf16[32,19,512]{2,1,0:T(8,128)(2,1)} %broadcast_in_dim.343), calls=%async_computation | async-start | bytes 1572864 | tf_op jit(solution)/shard_map/all_to_all | solution.py:33
  155.2 14.1 %copy-start.10 = (f32[3,512]{1,0:T(4,128)}, f32[3,512]{1,0:T(4,128)S(1)}, u32[]{:S(2)}) copy-start(f32[3,512]{1,0:T(4,128)S(1)} %get-tuple-element.435) | copy-start | bytes 18436
  155.2 14.1 %copy-start.12 = (f32[3,512]{1,0:T(4,128)}, f32[3,512]{1,0:T(4,128)S(1)}, u32[]{:S(2)}) copy-start(f32[3,512]{1,0:T(4,128)S(1)} %get-tuple-element.436) | copy-start | bytes 18436
  155.3 14.1 %copy-start.14 = (f32[3,512]{1,0:T(4,128)}, f32[3,512]{1,0:T(4,128)S(1)}, u32[]{:S(2)}) copy-start(f32[3,512]{1,0:T(4,128)S(1)} %get-tuple-element.437) | copy-start | bytes 18436
  155.3 14.1 %copy-start.16 = (f32[3,512]{1,0:T(4,128)}, f32[3,512]{1,0:T(4,128)S(1)}, u32[]{:S(2)}) copy-start(f32[3,512]{1,0:T(4,128)S(1)} %get-tuple-element.438) | copy-start | bytes 18436
  155.3 14.1 %copy-start.18 = (f32[3,512]{1,0:T(4,128)}, f32[3,512]{1,0:T(4,128)S(1)}, u32[]{:S(2)}) copy-start(f32[3,512]{1,0:T(4,128)S(1)} %get-tuple-element.439) | copy-start | bytes 18436
  155.3 14.1 %copy-start.20 = (f32[3,512]{1,0:T(4,128)}, f32[3,512]{1,0:T(4,128)S(1)}, u32[]{:S(2)}) copy-start(f32[3,512]{1,0:T(4,128)S(1)} %get-tuple-element.440) | copy-start | bytes 18436
  159.3 4.5 copy-start.54
  162.5 3.5 copy-start.53
  162.9 0.7 copy-start.5
  163.6 3.4 copy-start.57
  163.7 4.3 copy-start.58
  166.9 4.3 copy-start.6
  166.9 4.3 copy-start.23
  169.3 2.2 copy-start.8
  171.2 26.5 %copy-start = (f32[3,320,512]{2,1,0:T(8,128)}, f32[3,320,512]{2,1,0:T(8,128)S(1)}, u32[]{:S(2)}) copy-start(f32[3,320,512]{2,1,0:T(8,128)S(1)} %fusion.5) | copy-start | bytes 5898244
  171.2 26.5 %copy-start.29 = (pred[127]{0:T(512)(128)(4,1)S(1)}, pred[127]{0:T(512)(128)(4,1)}, u32[]{:S(2)}) copy-start(pred[127]{0:T(512)(128)(4,1)} %iota_compare_fusion.30) | copy-start | bytes 385
  171.3 26.6 %copy-start.49 = (pred[127]{0:T(512)(128)(4,1)S(1)}, pred[127]{0:T(512)(128)(4,1)}, u32[]{:S(2)}) copy-start(pred[127]{0:T(512)(128)(4,1)} %iota_compare_fusion.31) | copy-start | bytes 385
  171.3 26.7 %copy-start.48 = (pred[127]{0:T(512)(128)(4,1)S(1)}, pred[127]{0:T(512)(128)(4,1)}, u32[]{:S(2)}) copy-start(pred[127]{0:T(512)(128)(4,1)} %iota_compare_fusion.32) | copy-start | bytes 385
  171.5 26.6 %copy-start.47 = (pred[127]{0:T(512)(128)(4,1)S(1)}, pred[127]{0:T(512)(128)(4,1)}, u32[]{:S(2)}) copy-start(pred[127]{0:T(512)(128)(4,1)} %iota_compare_fusion.33) | copy-start | bytes 385
  171.5 26.7 %copy-start.46 = (pred[127]{0:T(512)(128)(4,1)S(1)}, pred[127]{0:T(512)(128)(4,1)}, u32[]{:S(2)}) copy-start(pred[127]{0:T(512)(128)(4,1)} %iota_compare_fusion.34) | copy-start | bytes 385
  171.5 26.9 %copy-start.45 = (pred[127]{0:T(512)(128)(4,1)S(1)}, pred[127]{0:T(512)(128)(4,1)}, u32[]{:S(2)}) copy-start(pred[127]{0:T(512)(128)(4,1)} %iota_compare_fusion.35) | copy-start | bytes 385
  171.5 27.0 %copy-start.44 = (pred[127]{0:T(512)(128)(4,1)S(1)}, pred[127]{0:T(512)(128)(4,1)}, u32[]{:S(2)}) copy-start(pred[127]{0:T(512)(128)(4,1)} %iota_compare_fusion.36) | copy-start | bytes 385
  171.6 27.0 %copy-start.30 = (pred[127]{0:T(512)(128)(4,1)S(1)}, pred[127]{0:T(512)(128)(4,1)}, u32[]{:S(2)}) copy-start(pred[127]{0:T(512)(128)(4,1)} %iota_compare_fusion.39) | copy-start | bytes 385
  197.8 13.8 %copy-start.32 = (pred[127]{0:T(512)(128)(4,1)S(1)}, pred[127]{0:T(512)(128)(4,1)}, u32[]{:S(2)}) copy-start(pred[127]{0:T(512)(128)(4,1)} %iota_compare_fusion.26) | copy-start | bytes 385
  197.8 13.9 %copy-start.50 = (pred[127]{0:T(512)(128)(4,1)S(1)}, pred[127]{0:T(512)(128)(4,1)}, u32[]{:S(2)}) copy-start(pred[127]{0:T(512)(128)(4,1)} %iota_compare_fusion.27) | copy-start | bytes 385
  197.9 13.9 %copy-start.52 = (pred[127]{0:T(512)(128)(4,1)S(1)}, pred[127]{0:T(512)(128)(4,1)}, u32[]{:S(2)}) copy-start(pred[127]{0:T(512)(128)(4,1)} %iota_compare_fusion.28) | copy-start | bytes 385
  198.0 13.9 %copy-start.56 = (pred[127]{0:T(512)(128)(4,1)S(1)}, pred[127]{0:T(512)(128)(4,1)}, u32[]{:S(2)}) copy-start(pred[127]{0:T(512)(128)(4,1)} %iota_compare_fusion.29) | copy-start | bytes 385
  198.3 13.9 %copy-start.43 = (pred[127]{0:T(512)(128)(4,1)S(1)}, pred[127]{0:T(512)(128)(4,1)}, u32[]{:S(2)}) copy-start(pred[127]{0:T(512)(128)(4,1)} %iota_compare_fusion.40) | copy-start | bytes 385
  198.3 13.9 %copy-start.51 = (pred[127]{0:T(512)(128)(4,1)S(1)}, pred[127]{0:T(512)(128)(4,1)}, u32[]{:S(2)}) copy-start(pred[127]{0:T(512)(128)(4,1)} %iota_compare_fusion.41) | copy-start | bytes 385
  212.6 156.8 %copy-start.27 = (pred[127]{0:T(512)(128)(4,1)S(1)}, pred[127]{0:T(512)(128)(4,1)}, u32[]{:S(2)}) copy-start(pred[127]{0:T(512)(128)(4,1)} %iota_compare_fusion.17) | copy-start | bytes 385
  212.6 156.8 %copy-start.34 = (pred[127]{0:T(512)(128)(4,1)S(1)}, pred[127]{0:T(512)(128)(4,1)}, u32[]{:S(2)}) copy-start(pred[127]{0:T(512)(128)(4,1)} %iota_compare_fusion.18) | copy-start | bytes 385
  343.0 26.6 %copy-start.35 = (pred[127]{0:T(512)(128)(4,1)S(1)}, pred[127]{0:T(512)(128)(4,1)}, u32[]{:S(2)}) copy-start(pred[127]{0:T(512)(128)(4,1)} %iota_compare_fusion.19) | copy-start | bytes 385
  343.0 26.7 %copy-start.36 = (pred[127]{0:T(512)(128)(4,1)S(1)}, pred[127]{0:T(512)(128)(4,1)}, u32[]{:S(2)}) copy-start(pred[127]{0:T(512)(128)(4,1)} %iota_compare_fusion.20) | copy-start | bytes 385
  343.0 26.9 %copy-start.37 = (pred[127]{0:T(512)(128)(4,1)S(1)}, pred[127]{0:T(512)(128)(4,1)}, u32[]{:S(2)}) copy-start(pred[127]{0:T(512)(128)(4,1)} %iota_compare_fusion.21) | copy-start | bytes 385
  343.0 27.0 %copy-start.38 = (pred[127]{0:T(512)(128)(4,1)S(1)}, pred[127]{0:T(512)(128)(4,1)}, u32[]{:S(2)}) copy-start(pred[127]{0:T(512)(128)(4,1)} %iota_compare_fusion.22) | copy-start | bytes 385
  343.0 27.1 %copy-start.39 = (pred[127]{0:T(512)(128)(4,1)S(1)}, pred[127]{0:T(512)(128)(4,1)}, u32[]{:S(2)}) copy-start(pred[127]{0:T(512)(128)(4,1)} %iota_compare_fusion.23) | copy-start | bytes 385
  343.1 27.2 %copy-start.28 = (pred[127]{0:T(512)(128)(4,1)S(1)}, pred[127]{0:T(512)(128)(4,1)}, u32[]{:S(2)}) copy-start(pred[127]{0:T(512)(128)(4,1)} %iota_compare_fusion.24) | copy-start | bytes 385
  369.6 13.7 %copy-start.31 = (pred[127]{0:T(512)(128)(4,1)S(1)}, pred[127]{0:T(512)(128)(4,1)}, u32[]{:S(2)}) copy-start(pred[127]{0:T(512)(128)(4,1)} %iota_compare_fusion.13) | copy-start | bytes 385
  369.6 13.7 %copy-start.40 = (pred[127]{0:T(512)(128)(4,1)S(1)}, pred[127]{0:T(512)(128)(4,1)}, u32[]{:S(2)}) copy-start(pred[127]{0:T(512)(128)(4,1)} %iota_compare_fusion.14) | copy-start | bytes 385
  369.8 13.7 %copy-start.41 = (pred[127]{0:T(512)(128)(4,1)S(1)}, pred[127]{0:T(512)(128)(4,1)}, u32[]{:S(2)}) copy-start(pred[127]{0:T(512)(128)(4,1)} %iota_compare_fusion.15) | copy-start | bytes 385
  369.9 13.7 %copy-start.55 = (pred[127]{0:T(512)(128)(4,1)S(1)}, pred[127]{0:T(512)(128)(4,1)}, u32[]{:S(2)}) copy-start(pred[127]{0:T(512)(128)(4,1)} %iota_compare_fusion.16) | copy-start | bytes 385
  370.2 13.7 %copy-start.42 = (pred[127]{0:T(512)(128)(4,1)S(1)}, pred[127]{0:T(512)(128)(4,1)}, u32[]{:S(2)}) copy-start(pred[127]{0:T(512)(128)(4,1)} %iota_compare_fusion.25) | copy-start | bytes 385
  516.2 1.7 copy-start.9
  517.9 2.1 copy-start.1
  517.9 2.1 copy-start.3
  517.9 2.7 copy-start.7
  793.1 8.6 copy-start.2
  793.1 8.6 copy-start.4
  794.1 21.1 %all-to-all-start.2 = ((f32[32,149,16]{1,2,0:T(8,128)}), f32[32,149,16]{1,2,0:T(8,128)S(1)}, u32[]{:S(2)}, u32[]{:S(2)}) async-start(f32[32,149,16]{1,2,0:T(8,128)} %maximum_bitcast_fusion), calls=%async_computation.2 | async-start | bytes 1048576 | tf_op jit(solution)/shard_map/all_to_all | solution.py:106
  816.1 61.8 %all-to-all-start.1 = ((bf16[32,19,512]{2,1,0:T(8,128)(2,1)}), bf16[32,19,512]{2,1,0:T(8,128)(2,1)S(1)}, u32[]{:S(2)}, u32[]{:S(2)}) async-start(bf16[32,19,512]{2,1,0:T(8,128)(2,1)} %broadcast_in_dim.377), calls=%async_computation.1 | async-start | bytes 1572864 | tf_op jit(solution)/shard_map/all_to_all | solution.py:33
  821.0 58.0 %copy-start.33 = (pred[32]{0:T(512)(128)(4,1)S(1)}, pred[32]{0:T(512)(128)(4,1)}, u32[]{:S(2)}) copy-start(pred[32]{0:T(512)(128)(4,1)} %get-tuple-element.433) | copy-start | bytes 100
  881.9 4.9 copy-start.11
  881.9 4.9 copy-start.13
  881.9 4.9 copy-start.15
  881.9 4.9 copy-start.17
  881.9 4.9 copy-start.19
  881.9 4.9 copy-start.21
  881.9 4.9 copy-start.24
where the time goes:
time: 907 us; the launch traced here: 890 us
  other arithmetic  325 us (36%)
  blocking collectives  217 us (24%)
  loops' own time  175 us (19%)
  local copies, waits for them, and re-layouts  111 us (12%)
  between operations  25.5 us (3%)
  starting transfers between devices  22.6 us (2%)
  waiting for transfers between devices  13.2 us (1%)
    another operation x1, loops' own time, tap_products(): return lax.map(one_tap, jnp.arange(taps, dtype=jnp.int32))  169 us
    mul x128, other arithmetic, causal_add_tap(): filt[tap_index].astype(jnp.float32)[None, :] * piece.astype(jnp.float32)  90.4 us
    mul x128, other arithmetic, anticausal_add_tap(): filt[tap_index].astype(jnp.float32)[None, :] * piece.astype(jnp.float32)  90.4 us
    all_gather x4, blocking collectives, entering(): pieces = jax.tree.map(lambda part: lax.all_gather(part, axis), running)  78 us
    dynamic_slice x128, local copies, waits for them, and re-layouts, tap_products(): return lax.map(one_tap, jnp.arange(taps, dtype=jnp.int32))  75 us
    psum x4, blocking collectives, over_axes(): return functools.reduce(lax.psum, axes, shard)  54.2 us
    all_gather x1, blocking collectives, rows_first(): result = lax.all_gather(both, axis, axis=0, tiled=True)  49.4 us
    add x128, other arithmetic, causal_add_tap(): total + filt[tap_index].astype(jnp.float32)[None, :] * piece.astype(jnp.f...  36.9 us
  transfers between devices with their start and end apart: 3, of which 1 were waited for; matrix products, arithmetic and copies ran while one was open for 4% of the time, Pallas kernels for 0%

commit v1 on v0

v1 whole, which is shorter than its diff:
```python
import jax
import jax.numpy as jnp
import numpy as np
from jax import lax
from jax.experimental import pallas as pl
from jax.experimental.pallas import tpu as pltpu
from jax.sharding import PartitionSpec as P

LTAP = 128
STAP = 7
BLK = 128
FREQ = 2 * BLK
DEAD = 2.0**100
F32 = jnp.float32
BF16 = jnp.bfloat16


def split_np(matrix):
    high = matrix.astype(jnp.bfloat16)
    low = (matrix - high.astype(np.float64)).astype(jnp.bfloat16)
    return high, low


def dft_tables():
    n = np.arange(BLK)[:, None]
    k = np.arange(BLK)[None, :]
    angle = 2.0 * np.pi * ((n * k) % FREQ) / FREQ
    cosines, sines = np.cos(angle), -np.sin(angle)
    nyquist = np.where(n % 2 == 0, 1.0, -1.0)
    sines[:, :1] = nyquist
    forward = np.concatenate([cosines, sines], axis=1)
    weight = np.full((FREQ, 1), 2.0 / FREQ)
    weight[0] = weight[BLK] = 1.0 / FREQ
    backward = forward.T * weight
    return split_np(forward), split_np(backward)


def split2(x):
    high = x.astype(BF16)
    return high, (x - high.astype(F32)).astype(BF16)


def mm(a, b):
    return jnp.dot(a, b, preferred_element_type=F32)


def mm_nt(a, b):
    return lax.dot_general(a, b, (((1,), (1,)), ((), ())), preferred_element_type=F32)


def identity(size):
    rows = lax.broadcasted_iota(jnp.int32, (size, size), 0)
    cols = lax.broadcasted_iota(jnp.int32, (size, size), 1)
    return jnp.where(rows == cols, 1.0, 0.0).astype(BF16)


def turn_out_kernel(count_ref, s_ref, d_ref, o_ref):
    slots = s_ref.shape[2]
    channels = s_ref.shape[3]
    count = count_ref[0, 0]
    wide = min(256, channels)
    eye = identity(wide)
    for part in range(4):
        for at in range(0, slots, 64):
            rows = s_ref[part, 0, at : at + 64, :] if part < 3 else d_ref[0, at : at + 64, :]
            lane = lax.broadcasted_iota(jnp.int32, (wide, 64), 1) + at
            for c in range(0, channels, wide):
                turned = mm_nt(eye, rows[:, c : c + wide])
                kept = jnp.where(lane < count, turned, 0.0 if part < 3 else DEAD)
                first = part * slots + at
                o_ref[c : c + wide, first : first + 64] = kept.astype(BF16)


def turn_back_kernel(count_ref, r_ref, o_ref):
    slots = o_ref.shape[2]
    channels = o_ref.shape[3]
    count = count_ref[0, 0]
    eye = identity(64)
    for part in range(3):
        for at in range(0, slots, 64):
            first = part * slots + at
            turned = mm_nt(eye, r_ref[:, first : first + 64])
            row = lax.broadcasted_iota(jnp.int32, (64, channels), 0) + at
            o_ref[part, 0, at : at + 64, :] = jnp.where(row < count, turned, 0.0).astype(BF16)


def core_kernel(
    off_ref, r_ref, h_ref, w_ref, fh_ref, fl_ref, gh_ref, gl_ref,
    o_ref, graw_ref,
    x_ref, k_ref, v_ref, z_ref, d_ref, az_ref, ad_ref, dm_ref, out_ref,
):
    pieces, chans, _ = r_ref.shape
    slots = r_ref.shape[2] // 4
    nb = z_ref.shape[0]
    lane = lax.broadcasted_iota(jnp.int32, (chans, BLK), 1)

    x_ref[...] = jnp.zeros(x_ref.shape, F32)

    def place(offset, part):
        aligned = part * slots // BLK * BLK
        base = offset - (part * slots - aligned)
        return aligned, lax.shift_right_arithmetic(base, 7) + 1, lax.bitwise_and(base, 127)

    def pack(j, carry):
        offset = off_ref[j]
        for part in range(4):
            aligned, block, turn = place(offset, part)
            skip = part * slots - aligned
            rolled = []
            for n in range(3):
                piece = r_ref[j, :, aligned + n * BLK : aligned + (n + 1) * BLK].astype(F32)
                if part == 3:
                    piece = jnp.where(piece > 2.0**50, 0.0, piece)
                if n * BLK < skip:
                    piece = jnp.where(lane >= skip - n * BLK, piece, 0.0)
                if (n + 1) * BLK > skip + slots:
                    piece = jnp.where(lane < skip + slots - n * BLK, piece, 0.0)
                rolled.append(pltpu.roll(piece, turn, 1))
            early = lane < turn
            x_ref[part, block] += jnp.where(early, 0.0, rolled[0])
            x_ref[part, block + 1] += jnp.where(early, rolled[0], rolled[1])
            x_ref[part, block + 2] += jnp.where(early, rolled[1], rolled[2])
            x_ref[part, block + 3] += jnp.where(early, rolled[2], 0.0)
        return carry

    lax.fori_loop(0, pieces, pack, 0)

    def features(b, carry):
        feats = []
        for m in range(3):
            before, here = x_ref[m, b], x_ref[m, b + 1]
            total = w_ref[m * STAP] * here
            for i in range(1, STAP):
                moved = pltpu.roll(jnp.where(lane >= BLK - i, before, here), i, 1)
                total = total + w_ref[m * STAP + i] * moved
            feats.append(total)
        k_ref[b] = feats[1]
        v_ref[b] = feats[2]
        z_ref[b] = (feats[1] * feats[2]).astype(BF16)
        d_ref[b] = (x_ref[3, b + 1] * feats[0]).astype(BF16)
        return carry

    lax.fori_loop(0, nb, features, 0)

    step = 16
    az_ref[0] = jnp.zeros((chans, FREQ), F32)
    ad_ref[nb] = jnp.zeros((chans, FREQ), F32)

    def spectra(c, carry):
        at = c * step
        zs = z_ref[pl.ds(at, step)].reshape(step * chans, BLK)
        ds = d_ref[pl.ds(at, step)].reshape(step * chans, BLK)
        fh, fl = fh_ref[...], fl_ref[...]
        az_ref[pl.ds(at + 1, step)] = (mm(zs, fh) + mm(zs, fl)).reshape(step, chans, FREQ)
        ad_ref[pl.ds(at, step)] = (mm(ds, fh) + mm(ds, fl)).reshape(step, chans, FREQ)
        return carry

    lax.fori_loop(0, nb // step, spectra, 0)

    sign = 1.0 - 2.0 * lax.bitwise_and(
        lax.broadcasted_iota(jnp.int32, (1, 1, FREQ), 2), 1
    ).astype(F32)
    chunk = 8

    def turn(re, im):
        spectrum = jnp.concatenate([re, im], axis=2).reshape(-1, FREQ)
        high, low = split2(spectrum)
        gh, gl = gh_ref[...], gl_ref[...]
        result = mm(high, gh) + (mm(low, gh) + mm(high, gl))
        return result.reshape(-1, chans, BLK)

    def long(c, carry):
        p1, p2, p3 = carry
        at = c * chunk
        hre, him, hny = h_ref[0][None], h_ref[1][None], h_ref[2][None]
        window = az_ref[pl.ds(at + 1, chunk)] + sign * az_ref[pl.ds(at, chunk)]
        zre, zim = window[:, :, :BLK], window[:, :, BLK:]
        own = ad_ref[pl.ds(at, chunk)]
        ore, oim = own[:, :, :BLK], own[:, :, BLK:]
        both = own + sign * ad_ref[pl.ds(at + 1, chunk)]
        dre, dim = both[:, :, :BLK], both[:, :, BLK:]
        y = turn(zre * hre - zim * him, zim * hny + zre * him)
        dz = turn(dre * hre + dim * him, dim * hny - dre * him)
        dm_ref[0, pl.ds(at, chunk)] = (x_ref[3, pl.ds(at + 1, chunk)] * y).astype(BF16).astype(F32)
        dm_ref[1, pl.ds(at, chunk)] = (dz * v_ref[pl.ds(at, chunk)]).astype(BF16).astype(F32)
        dm_ref[2, pl.ds(at, chunk)] = (dz * k_ref[pl.ds(at, chunk)]).astype(BF16).astype(F32)
        p1 = p1 + jnp.sum(ore * zre, axis=0)
        p2 = p2 + jnp.sum(oim * zim, axis=0)
        p3 = p3 + jnp.sum(oim * zre - ore * zim, axis=0)
        return p1, p2, p3

    zero = jnp.zeros((chans, BLK), F32)
    p1, p2, p3 = lax.fori_loop(0, nb // chunk, long, (zero, zero, zero))
    lre = p1 + jnp.where(lane == 0, 0.0, p2)
    lim = jnp.where(lane == 0, p2, p3)
    graw_ref[0] = turn(lre[None], lim[None])[0]

    dm_ref[:, nb] = jnp.zeros((3, chans, BLK), F32)
    out_ref[:, 0] = jnp.zeros((3, chans, BLK), F32)
    for extra in range(nb + 1, out_ref.shape[1]):
        out_ref[:, extra] = jnp.zeros((3, chans, BLK), F32)
    shorts = zero
    for m in range(3):

        def back(b, sums, m=m):
            here, after, stream = dm_ref[m, b], dm_ref[m, b + 1], x_ref[m, b + 1]
            total = w_ref[m * STAP] * here
            fresh = [sums[0] + stream * here]
            for i in range(1, STAP):
                moved = pltpu.roll(jnp.where(lane < i, after, here), BLK - i, 1)
                total = total + w_ref[m * STAP + i] * moved
                fresh.append(sums[i] + stream * moved)
            out_ref[m, b + 1] = total
            return tuple(fresh)

        sums = lax.fori_loop(0, nb, back, (zero,) * STAP)
        for i in range(STAP):
            column = jnp.sum(sums[i], axis=1, keepdims=True)
            shorts = jnp.where(lane == m * STAP + i, column, shorts)
    graw_ref[1] = shorts

    def unpack(j, carry):
        offset = off_ref[j]
        kept = []
        for part in range(3):
            aligned, block, turned = place(offset, part)
            back_by = lax.bitwise_and(BLK - turned, 127)
            early = lane < turned
            for n in range(3):
                both = jnp.where(early, out_ref[part, block + n + 1], out_ref[part, block + n])
                kept.append(pltpu.roll(both, back_by, 1))
        shared = jnp.where(lane < 64, kept[2], kept[3])
        blocks = [kept[0], kept[1], shared, kept[4], kept[5], kept[6], kept[7], kept[8]]
        for n, block in enumerate(blocks):
            o_ref[j, :, n * BLK : (n + 1) * BLK] = block.astype(BF16)
        return carry

    lax.fori_loop(0, pieces, unpack, 0)


def solution(mesh):
    ctx = mesh.shape["ctx"]
    everyone = mesh.size
    (fh, fl), (gh, gl) = dft_tables()
    smem = pl.BlockSpec(memory_space=pltpu.SMEM)
    vmem = pl.BlockSpec(memory_space=pltpu.VMEM)

    def local(streams, cotangent, counts, short_filters, long_filter):
        slots, channels = streams.shape[2:]
        own = channels // ctx
        length = 8192
        nb = length // BLK
        total_params = float((LTAP + 3 * STAP) * channels * mesh.shape["dp"])

        turned = pl.pallas_call(
            turn_out_kernel,
            out_shape=jax.ShapeDtypeStruct((channels, 4 * slots), BF16),
            in_specs=[smem, vmem, vmem],
            out_specs=vmem,
            name="turn_out",
        )(counts, streams, cotangent)
        pieces = lax.all_to_all(
            turned.reshape(ctx, own, 4 * slots), "ctx", 0, 0, tiled=True
        )
        marks = pieces[:, 0, 3 * slots :].astype(F32) < 2.0**50
        live = jnp.sum(marks.astype(jnp.int32), axis=1)
        order = jnp.arange(ctx, dtype=jnp.int32)
        offsets = jnp.sum(jnp.where(order[None, :] < order[:, None], live[None, :], 0), axis=1)

        taps = long_filter.T
        spectrum = mm(taps, jnp.asarray(fh)) + mm(taps, jnp.asarray(fl))
        first = jnp.arange(BLK)[None, :] == 0
        hre, him = spectrum[:, :BLK], spectrum[:, BLK:]
        filters = jnp.stack([hre, jnp.where(first, 0.0, him), jnp.where(first, him, hre)])
        weights = jnp.broadcast_to(
            short_filters.reshape(3 * STAP, own, 1).astype(F32), (3 * STAP, own, BLK)
        )

        padded = nb + 4
        grads, raw = pl.pallas_call(
            core_kernel,
            out_shape=(
                jax.ShapeDtypeStruct((ctx, own, 8 * BLK), BF16),
                jax.ShapeDtypeStruct((2, own, BLK), F32),
            ),
            in_specs=[smem] + [vmem] * 7,
            out_specs=(vmem, vmem),
            scratch_shapes=[
                pltpu.VMEM((4, padded, own, BLK), F32),
                pltpu.VMEM((nb, own, BLK), F32),
                pltpu.VMEM((nb, own, BLK), F32),
                pltpu.VMEM((nb, own, BLK), BF16),
                pltpu.VMEM((nb, own, BLK), BF16),
                pltpu.VMEM((nb + 1, own, FREQ), F32),
                pltpu.VMEM((nb + 1, own, FREQ), F32),
                pltpu.VMEM((3, nb + 1, own, BLK), F32),
                pltpu.VMEM((3, padded, own, BLK), F32),
            ],
            compiler_params=pltpu.CompilerParams(vmem_limit_bytes=40 << 20),
            name="core",
        )(
            offsets, pieces, filters, weights,
            jnp.asarray(fh), jnp.asarray(fl), jnp.asarray(gh), jnp.asarray(gl),
        )

        squares = jnp.sum(raw * raw)
        shared = lax.all_to_all(
            jnp.broadcast_to(squares, (everyone, 1, BLK)), ("dp", "ctx"), 0, 0, tiled=True
        )
        back = lax.all_to_all(grads, "ctx", 0, 0, tiled=True)
        stream_grads = pl.pallas_call(
            turn_back_kernel,
            out_shape=jax.ShapeDtypeStruct((3, 1, slots, channels), BF16),
            in_specs=[smem, vmem],
            out_specs=vmem,
            name="turn_back",
        )(counts, back.reshape(channels, 8 * BLK))

        rms = jnp.sqrt(jnp.sum(shared[:, 0, 0]) / total_params + 1e-06)
        long_grad = (raw[0] / rms).T
        short_grad = (raw[1, :, : 3 * STAP] / rms).T.reshape(3, STAP, own)
        return stream_grads, long_grad, short_grad

    return jax.shard_map(
        local,
        mesh=mesh,
        in_specs=(
            P(None, None, "ctx", "dp"),
            P(None, "ctx", "dp"),
            P(None, "ctx"),
            P(None, None, ("dp", "ctx")),
            P(None, ("dp", "ctx")),
        ),
        out_specs=(
            P(None, None, "ctx", "dp"),
            P(None, ("dp", "ctx")),
            P(None, None, ("dp", "ctx")),
        ),
        check_vma=False,
    )
```

time: 907 us -> 157 us (0.17); the launches traced: 890 us -> 156 us
  other arithmetic: 325 us -> 3.26 us
  blocking collectives: 217 us -> 32.8 us
  loops' own time: 175 us -> 0 us
  local copies, waits for them, and re-layouts: 111 us -> 2.6 us
  waiting for transfers between devices: 13.2 us -> 58.9 us
  Pallas kernels: 0 us -> 40.9 us
  between operations: 25.5 us -> 2.12 us
    mul x257 -> x0, other arithmetic: 181 us -> none  [the longest x128 90.4 us: causal_add_tap(): filt[tap_index].astype(jnp.float32)[None, :] * piece.astype(jnp.float32)]
    another operation x3 -> x0, loops' own time: 175 us -> none  [the longest x1 169 us: tap_products(): return lax.map(one_tap, jnp.arange(taps, dtype=jnp.int32))]
    all_gather x5 -> x0, blocking collectives: 127 us -> none  [the longest x4 78 us: entering(): pieces = jax.tree.map(lambda part: lax.all_gather(part, axis), running)]
    add x257 -> x0, other arithmetic: 75.6 us -> none  [the longest x128 36.9 us: causal_add_tap(): total + filt[tap_index].astype(jnp.float32)[None, :] * piece.astype(jnp.f...]
    dynamic_slice x129 -> x0, local copies, waits for them, and re-layouts: 75.1 us -> none  [the longest x128 75 us: tap_products(): return lax.map(one_tap, jnp.arange(taps, dtype=jnp.int32))]
    psum x4 -> x0, blocking collectives: 54.2 us -> none  [over_axes(): return functools.reduce(lax.psum, axes, shard)]
    all_to_all x3 -> x2, waiting for transfers between devices: 13.2 us -> 58.9 us  [the longest x1 33.6 us: local(): lax.all_to_all(turned.reshape(ctx, own, 4 * slots), 'ctx', 0, 0, tiled=True)]
    pallas_call x0 -> x3, Pallas kernels: none -> 40.9 us  [the longest x1 34 us: local(): pl.pallas_call(core_kernel, out_shape=(jax.ShapeDtypeStruct((ctx, own, 8...]
  transfers between devices with their start and end apart: 3 -> 2, of which waited for: 1 -> 2; matrix products, arithmetic and copies ran while one was open for 4% -> 2% of each run, Pallas kernels for 0% -> 0%
where the time goes in v1:
time: 157 us; the launch traced here: 156 us
  waiting for transfers between devices  58.9 us (38%)
  Pallas kernels  40.9 us (26%)
  blocking collectives  32.8 us (21%)
  starting transfers between devices  15.3 us (10%)
  other arithmetic  3.26 us (2%)
  local copies, waits for them, and re-layouts  2.6 us (2%)
  between operations  2.12 us (1%)
    pallas_call x1, Pallas kernels, local(): pl.pallas_call(core_kernel, out_shape=(jax.ShapeDtypeStruct((ctx, own, 8...  34 us
    all_to_all x1, waiting for transfers between devices, local(): lax.all_to_all(turned.reshape(ctx, own, 4 * slots), 'ctx', 0, 0, tiled=True)  33.6 us
    all_to_all x1, blocking collectives, local(): lax.all_to_all(jnp.broadcast_to(squares, (everyone, 1, BLK)), ('dp', 'ctx...  32.8 us
    all_to_all x1, waiting for transfers between devices, local(): back = lax.all_to_all(grads, 'ctx', 0, 0, tiled=True)  25.3 us
    all_to_all x1, starting transfers between devices, local(): lax.all_to_all(turned.reshape(ctx, own, 4 * slots), 'ctx', 0, 0, tiled=True)  10.3 us
    all_to_all x1, starting transfers between devices, local(): back = lax.all_to_all(grads, 'ctx', 0, 0, tiled=True)  4.96 us
    pallas_call x1, Pallas kernels, local(): pl.pallas_call(turn_out_kernel, out_shape=jax.ShapeDtypeStruct((channels,...  3.92 us
  transfers between devices with their start and end apart: 2, of which 2 were waited for; matrix products, arithmetic and copies ran while one was open for 2% of the time, Pallas kernels for 0%

profile of v1, /device:TPU:8, one launch (start us, length us, event | category | flops | bytes accessed | tf_op | source)
XLA Modules:
  0.0 156.0 jit_solution(17373053473591419101)
XLA Ops:
  0.6 0.0 copy-start
  1.3 3.9 %turn_out.1 = bf16[512,1280]{1,0:T(8,128)(2,1)} custom-call(s32[1,1]{1,0:T(1,128)S(6)} %copy.20.count_ref, bf16[3,1,320,512]{3,2,1,0:T(8,128)(2,1)} %s_ref.1, bf16[1,320,512]{2,1,0:T(8,128)(2,1)} %d_ref.1), custom_call_target="tpu_custom_call" | custom-call | tf_op jit(solution)/shard_map/turn_out/pallas_call | solution.py:255
  5.2 0.0 copy-start.6
  5.2 0.0 copy-start.1
  5.2 0.0 copy-start.2
  5.2 0.0 copy-start.3
  5.2 0.0 copy-start.4
  5.3 10.3 %all-to-all-start = ((bf16[32,16,1280]{2,1,0:T(8,128)(2,1)}), bf16[32,16,1280]{2,1,0:T(8,128)(2,1)S(1)}, u32[]{:S(2)}, u32[]{:S(2)}) async-start(bf16[32,16,1280]{2,1,0:T(8,128)(2,1)} %bitcast.22), calls=%async_computation | async-start | bytes 2621440 | tf_op jit(solution)/shard_map/all_to_all | solution.py:262
  15.6 0.0 copy-done.6
  15.6 0.0 copy-done
  15.6 0.0 copy-done.1
  15.6 0.1 fusion.2
  15.7 0.0 copy-done.2
  15.8 0.1 fusion
  15.9 33.6 %all-to-all-done.r_ref = bf16[32,16,1280]{2,1,0:T(8,128)(2,1)S(1)} async-done(((bf16[32,16,1280]{2,1,0:T(8,128)(2,1)}), bf16[32,16,1280]{2,1,0:T(8,128)(2,1)S(1)}, u32[]{:S(2)}, u32[]{:S(2)}) %all-to-all-start) | async-done | bytes 1310752 | tf_op jit(solution)/shard_map/all_to_all | solution.py:262
  49.5 0.8 fusion.1
  50.3 0.1 select_reduce_fusion.off_ref
  50.4 0.1 broadcast_in_dim.48.w_ref
  50.5 0.0 copy-done.3
  50.5 0.0 copy-done.4
  50.5 34.0 %core.1 = (bf16[32,16,1024]{2,1,0:T(8,128)(2,1)}, f32[2,16,128]{2,1,0:T(8,128)S(1)}) custom-call(s32[32]{0:T(128)S(1)} %select_reduce_fusion.off_ref, bf16[32,16,1280]{2,1,0:T(8,128)(2,1)S(1)} %all-to-all-done.r_ref, f32[3,16,128]{2,1,0:T(8,128)S(1)} %pad_maximum_fusion.h_ref, f32[21,16,128]{2,1,0:T(8,128)S(1)} %broadcast_in_dim.48.w_ref, ...), custom_call_target="tpu_custom_call" | custom-call | tf_op jit(solution)/shard_map/core/pallas_call | solution.py:280
  84.5 0.6 multiply_reduce_fusion
  85.1 0.8 broadcast_in_dim.49
  85.9 32.8 %all_to_all.15 = f32[512,1,128]{2,1,0:T(1,128)S(1)} all-to-all(f32[512,1,128]{2,1,0:T(1,128)S(1)} %broadcast_in_dim.49), channel_id=1, replica_groups=mesh['dp'=16,'ctx'=32] {'dp','ctx'}, dimensions={0} | all-to-all | bytes 524288 | tf_op jit(solution)/shard_map/all_to_all | solution.py:307
  118.6 5.0 %all-to-all-start.1 = ((bf16[32,16,1024]{2,1,0:T(8,128)(2,1)}), bf16[32,16,1024]{2,1,0:T(8,128)(2,1)S(1)}, u32[]{:S(2)}, u32[]{:S(2)}) async-start(bf16[32,16,1024]{2,1,0:T(8,128)(2,1)} %get-tuple-element.5), calls=%async_computation.1 | async-start | bytes 2097152 | tf_op jit(solution)/shard_map/all_to_all | solution.py:310
  123.6 1.1 slice_reduce_fusion
  125.4 0.1 copy.18
  125.5 0.6 reshape.41
  126.1 0.6 divide_bitcast_fusion.1
  126.7 25.3 %all-to-all-done.1 = bf16[32,16,1024]{2,1,0:T(8,128)(2,1)S(1)} async-done(((bf16[32,16,1024]{2,1,0:T(8,128)(2,1)}), bf16[32,16,1024]{2,1,0:T(8,128)(2,1)S(1)}, u32[]{:S(2)}, u32[]{:S(2)}) %all-to-all-start.1) | async-done | bytes 1048608 | tf_op jit(solution)/shard_map/all_to_all | solution.py:310
  152.0 0.0 copy-start.5
  152.0 1.0 copy-done.5
  153.0 3.0 %turn_back.1 = bf16[3,1,320,512]{3,2,1,0:T(8,128)(2,1)} custom-call(s32[1,1]{1,0:T(1,128)S(6)} %copy.20.count_ref, bf16[512,1024]{1,0:T(8,128)(2,1)} %bitcast.23), custom_call_target="tpu_custom_call" | custom-call | tf_op jit(solution)/shard_map/turn_back/pallas_call | solution.py:311
  (5 shorter events, 0.0 us)
Async XLA Ops:
  0.6 15.0 %copy-start = (bf16[128,16]{0,1:T(8,128)(2,1)S(1)}, bf16[128,16]{0,1:T(8,128)(2,1)}, u32[]{:S(2)}) copy-start(bf16[128,16]{0,1:T(8,128)(2,1)} %param.13) | copy-start | bytes 12292
  5.2 10.3 %copy-start.6 = (bf16[3,7,16]{2,1,0:T(8,128)(2,1)S(1)}, bf16[3,7,16]{2,1,0:T(8,128)(2,1)}, u32[]{:S(2)}) copy-start(bf16[3,7,16]{2,1,0:T(8,128)(2,1)} %param.12) | copy-start | bytes 2020
  5.2 10.4 %copy-start.1 = (bf16[128,256]{1,0:T(8,128)(2,1)S(1)}, bf16[128,256]{1,0:T(8,128)(2,1)}, u32[]{:S(2)}) copy-start(bf16[128,256]{1,0:T(8,128)(2,1)} %constant.20.clone.fh_ref) | copy-start | bytes 196612
  5.2 10.5 %copy-start.2 = (bf16[128,256]{1,0:T(8,128)(2,1)S(1)}, bf16[128,256]{1,0:T(8,128)(2,1)}, u32[]{:S(2)}) copy-start(bf16[128,256]{1,0:T(8,128)(2,1)} %constant.21.clone.fl_ref) | copy-start | bytes 196612
  5.2 45.3 %copy-start.3 = (bf16[256,128]{1,0:T(8,128)(2,1)S(1)}, bf16[256,128]{1,0:T(8,128)(2,1)}, u32[]{:S(2)}) copy-start(bf16[256,128]{1,0:T(8,128)(2,1)} %constant.22.clone.gh_ref) | copy-start | bytes 196612
  5.2 45.3 %copy-start.4 = (bf16[256,128]{1,0:T(8,128)(2,1)S(1)}, bf16[256,128]{1,0:T(8,128)(2,1)}, u32[]{:S(2)}) copy-start(bf16[256,128]{1,0:T(8,128)(2,1)} %constant.23.clone.gl_ref) | copy-start | bytes 196612
  5.3 44.2 %all-to-all-start = ((bf16[32,16,1280]{2,1,0:T(8,128)(2,1)}), bf16[32,16,1280]{2,1,0:T(8,128)(2,1)S(1)}, u32[]{:S(2)}, u32[]{:S(2)}) async-start(bf16[32,16,1280]{2,1,0:T(8,128)(2,1)} %bitcast.22), calls=%async_computation | async-start | bytes 2621440 | tf_op jit(solution)/shard_map/all_to_all | solution.py:262
  118.6 33.4 %all-to-all-start.1 = ((bf16[32,16,1024]{2,1,0:T(8,128)(2,1)}), bf16[32,16,1024]{2,1,0:T(8,128)(2,1)S(1)}, u32[]{:S(2)}, u32[]{:S(2)}) async-start(bf16[32,16,1024]{2,1,0:T(8,128)(2,1)} %get-tuple-element.5), calls=%async_computation.1 | async-start | bytes 2097152 | tf_op jit(solution)/shard_map/all_to_all | solution.py:310
  152.0 1.0 copy-start.5

commit v2 on v1

v2 whole, which is shorter than its diff:
```python
import jax
import jax.numpy as jnp
import numpy as np
from jax import lax
from jax.experimental import pallas as pl
from jax.experimental.pallas import tpu as pltpu
from jax.sharding import Mesh
from jax.sharding import PartitionSpec as P

LTAP = 128
STAP = 7
BLK = 128
FREQ = 2 * BLK
DEAD = 2.0**100
F32 = jnp.float32
BF16 = jnp.bfloat16
DP = ("z", "core")
CTX = ("x", "y")


def split_np(matrix):
    high = matrix.astype(jnp.bfloat16)
    low = (matrix - high.astype(np.float64)).astype(jnp.bfloat16)
    return high, low


def dft_tables():
    n = np.arange(BLK)[:, None]
    k = np.arange(BLK)[None, :]
    angle = 2.0 * np.pi * ((n * k) % FREQ) / FREQ
    cosines, sines = np.cos(angle), -np.sin(angle)
    nyquist = np.where(n % 2 == 0, 1.0, -1.0)
    sines[:, :1] = nyquist
    forward = np.concatenate([cosines, sines], axis=1)
    weight = np.full((FREQ, 1), 2.0 / FREQ)
    weight[0] = weight[BLK] = 1.0 / FREQ
    backward = forward.T * weight
    return split_np(forward), split_np(backward)


def split2(x):
    high = x.astype(BF16)
    return high, (x - high.astype(F32)).astype(BF16)


def mm(a, b):
    return jnp.dot(a, b, preferred_element_type=F32)


def mm_nt(a, b):
    return lax.dot_general(a, b, (((1,), (1,)), ((), ())), preferred_element_type=F32)


def identity(size):
    rows = lax.broadcasted_iota(jnp.int32, (size, size), 0)
    cols = lax.broadcasted_iota(jnp.int32, (size, size), 1)
    return jnp.where(rows == cols, 1.0, 0.0).astype(BF16)


def turn_out_kernel(count_ref, s_ref, d_ref, o_ref):
    slots = s_ref.shape[2]
    channels = s_ref.shape[3]
    count = count_ref[0, 0]
    wide = min(256, channels)
    eye = identity(wide)
    for part in range(4):
        for at in range(0, slots, 64):
            rows = s_ref[part, 0, at : at + 64, :] if part < 3 else d_ref[0, at : at + 64, :]
            lane = lax.broadcasted_iota(jnp.int32, (wide, 64), 1) + at
            for c in range(0, channels, wide):
                turned = mm_nt(eye, rows[:, c : c + wide])
                kept = jnp.where(lane < count, turned, 0.0 if part < 3 else DEAD)
                first = part * slots + at
                o_ref[c : c + wide, first : first + 64] = kept.astype(BF16)


def turn_back_kernel(count_ref, r_ref, o_ref):
    slots = o_ref.shape[2]
    channels = o_ref.shape[3]
    count = count_ref[0, 0]
    eye = identity(64)
    for part in range(3):
        for at in range(0, slots, 64):
            first = part * slots + at
            turned = mm_nt(eye, r_ref[:, first : first + 64])
            row = lax.broadcasted_iota(jnp.int32, (64, channels), 0) + at
            o_ref[part, 0, at : at + 64, :] = jnp.where(row < count, turned, 0.0).astype(BF16)


def core_kernel(
    off_ref, r_ref, h_ref, w_ref, f_ref, g_ref,
    o_ref, graw_ref,
    x_ref, k_ref, v_ref, z_ref, d_ref, az_ref, ad_ref, dm_ref, out_ref,
):
    pieces, chans, _ = r_ref.shape
    slots = r_ref.shape[2] // 4
    nb = z_ref.shape[0]
    lane = lax.broadcasted_iota(jnp.int32, (chans, BLK), 1)

    none = jnp.zeros((chans, BLK), BF16)
    x_ref[...] = jnp.zeros(x_ref.shape, BF16)

    def place(offset, part):
        aligned = part * slots // BLK * BLK
        base = offset - (part * slots - aligned)
        return aligned, lax.shift_right_arithmetic(base, 7) + 1, lax.bitwise_and(base, 127)

    def pack(j, carry):
        offset = off_ref[j]
        for part in range(4):
            aligned, block, turn = place(offset, part)
            skip = part * slots - aligned
            rolled = []
            for n in range(3):
                piece = r_ref[j, :, aligned + n * BLK : aligned + (n + 1) * BLK]
                if part == 3:
                    piece = jnp.where(piece > 2.0**50, none, piece)
                if n * BLK < skip:
                    piece = jnp.where(lane >= skip - n * BLK, piece, none)
                if (n + 1) * BLK > skip + slots:
                    piece = jnp.where(lane < skip + slots - n * BLK, piece, none)
                rolled.append(pltpu.roll(piece, turn, 1))
            early = lane < turn
            x_ref[part, block] += jnp.where(early, none, rolled[0])
            x_ref[part, block + 1] += jnp.where(early, rolled[0], rolled[1])
            x_ref[part, block + 2] += jnp.where(early, rolled[1], rolled[2])
            x_ref[part, block + 3] += jnp.where(early, rolled[2], none)
        return carry

    lax.fori_loop(0, pieces, pack, 0, unroll=2)

    def later(before, here, i):
        return pltpu.roll(jnp.where(lane >= BLK - i, before, here), i, 1)

    def sooner(here, after, i):
        return pltpu.roll(jnp.where(lane < i, after, here), BLK - i, 1)

    def weighted(m, first, moved):
        total = w_ref[m * STAP + first] * moved[0]
        for i in range(1, min(len(moved), STAP - first)):
            total = total + w_ref[m * STAP + first + i] * moved[i]
        return total

    zero = jnp.zeros((chans, BLK), F32)

    def features(b, carried):
        feats, kept = [], []
        for m in range(3):
            before, here = x_ref[m, b], x_ref[m, b + 1]
            moved = [here.astype(F32)] + [later(before, here, i).astype(F32) for i in (1, 2, 3)]
            far = weighted(m, 4, moved)
            feats.append(weighted(m, 0, moved) + later(carried[m], far, 4))
            kept.append(far)
        k_ref[b] = feats[1]
        v_ref[b] = feats[2]
        z_ref[b] = (feats[1] * feats[2]).astype(BF16)
        d_ref[b] = (x_ref[3, b + 1].astype(F32) * feats[0]).astype(BF16)
        return tuple(kept)

    lax.fori_loop(0, nb, features, (zero,) * 3, unroll=4)

    step = 16
    az_ref[0] = jnp.zeros((chans, FREQ), F32)
    ad_ref[nb] = jnp.zeros((chans, FREQ), F32)

    def spectra(c, carry):
        at = c * step
        zs = z_ref[pl.ds(at, step)].reshape(step * chans, BLK)
        ds = d_ref[pl.ds(at, step)].reshape(step * chans, BLK)
        table = f_ref[...]
        for source, to, first in ((zs, az_ref, at + 1), (ds, ad_ref, at)):
            result = mm(jnp.concatenate([source, source], axis=1), table)
            to[pl.ds(first, step)] = result.reshape(step, chans, FREQ)
        return carry

    lax.fori_loop(0, nb // step, spectra, 0)

    sign = 1.0 - 2.0 * lax.bitwise_and(
        lax.broadcasted_iota(jnp.int32, (1, 1, FREQ), 2), 1
    ).astype(F32)
    chunk = 8

    def turn(re, im):
        rehi, relo = split2(re.reshape(-1, BLK))
        imhi, imlo = split2(im.reshape(-1, BLK))
        wide = jnp.concatenate([rehi, imhi, relo, imlo, rehi, imhi], axis=1)
        return mm(wide, g_ref[...]).reshape(-1, chans, BLK)

    def long(c, carry):
        p1, p2, p3 = carry
        at = c * chunk
        hre, him, hny = h_ref[0][None], h_ref[1][None], h_ref[2][None]
        window = az_ref[pl.ds(at + 1, chunk)] + sign * az_ref[pl.ds(at, chunk)]
        zre, zim = window[:, :, :BLK], window[:, :, BLK:]
        own = ad_ref[pl.ds(at, chunk)]
        ore, oim = own[:, :, :BLK], own[:, :, BLK:]
        p1 = p1 + jnp.sum(ore * zre, axis=0)
        p2 = p2 + jnp.sum(oim * zim, axis=0)
        p3 = p3 + jnp.sum(oim * zre - ore * zim, axis=0)
        y = turn(zre * hre - zim * him, zim * hny + zre * him)
        dm_ref[0, pl.ds(at, chunk)] = (x_ref[3, pl.ds(at + 1, chunk)].astype(F32) * y).astype(BF16)
        both = own + sign * ad_ref[pl.ds(at + 1, chunk)]
        dre, dim = both[:, :, :BLK], both[:, :, BLK:]
        dz = turn(dre * hre + dim * him, dim * hny - dre * him)
        dm_ref[1, pl.ds(at, chunk)] = (dz * v_ref[pl.ds(at, chunk)]).astype(BF16)
        dm_ref[2, pl.ds(at, chunk)] = (dz * k_ref[pl.ds(at, chunk)]).astype(BF16)
        return p1, p2, p3

    p1, p2, p3 = lax.fori_loop(0, nb // chunk, long, (zero, zero, zero))
    lre = p1 + jnp.where(lane == 0, 0.0, p2)
    lim = jnp.where(lane == 0, p2, p3)
    graw_ref[0] = turn(lre[None], lim[None])[0]

    dm_ref[:, nb] = jnp.zeros((3, chans, BLK), BF16)
    out_ref[:, 0] = jnp.zeros((3, chans, BLK), BF16)
    for extra in range(nb + 1, out_ref.shape[1]):
        out_ref[:, extra] = jnp.zeros((3, chans, BLK), BF16)
    shorts = zero
    for m in range(3):

        def back(n, carried, m=m):
            sums, far_after = carried
            b = nb - 1 - n
            here, after, stream = dm_ref[m, b], dm_ref[m, b + 1], x_ref[m, b + 1]
            old = later(x_ref[m, b], stream, 4).astype(F32)
            stream = stream.astype(F32)
            moved = [here.astype(F32)] + [sooner(here, after, i).astype(F32) for i in (1, 2, 3)]
            far = weighted(m, 4, moved)
            out_ref[m, b + 1] = (weighted(m, 0, moved) + sooner(far, far_after, 4)).astype(BF16)
            fresh = [sums[i] + stream * moved[i] for i in range(4)]
            fresh += [sums[4 + i] + old * moved[i] for i in range(3)]
            return tuple(fresh), far

        sums, _ = lax.fori_loop(0, nb, back, ((zero,) * STAP, zero), unroll=4)
        for i in range(STAP):
            column = jnp.sum(sums[i], axis=1, keepdims=True)
            shorts = jnp.where(lane == m * STAP + i, column, shorts)
    graw_ref[1] = shorts

    def unpack(j, carry):
        offset = off_ref[j]
        kept = []
        for part in range(3):
            aligned, block, turned = place(offset, part)
            back_by = lax.bitwise_and(BLK - turned, 127)
            early = lane < turned
            for n in range(3):
                both = jnp.where(early, out_ref[part, block + n + 1], out_ref[part, block + n])
                kept.append(pltpu.roll(both, back_by, 1))
        shared = jnp.where(lane < 64, kept[2], kept[3])
        blocks = [kept[0], kept[1], shared, kept[4], kept[5], kept[6], kept[7], kept[8]]
        for n, block in enumerate(blocks):
            o_ref[j, :, n * BLK : (n + 1) * BLK] = block
        return carry

    lax.fori_loop(0, pieces, unpack, 0, unroll=2)


def solution(mesh):
    ctx = mesh.shape["ctx"]
    cores = min(2, mesh.shape["dp"])
    finer = Mesh(mesh.devices.reshape(-1, cores, 4, ctx // 4), ("z", "core", "x", "y"))
    (fh, fl), (gh, gl) = dft_tables()
    forward = np.concatenate([fh, fl])
    backward = np.concatenate([gh, gh, gl])
    smem = pl.BlockSpec(memory_space=pltpu.SMEM)
    vmem = pl.BlockSpec(memory_space=pltpu.VMEM)

    def local(streams, cotangent, counts, short_filters, long_filter):
        slots, channels = streams.shape[2:]
        own = channels // ctx
        length = 8192
        nb = length // BLK
        total_params = float((LTAP + 3 * STAP) * channels * mesh.shape["dp"])

        turned = pl.pallas_call(
            turn_out_kernel,
            out_shape=jax.ShapeDtypeStruct((channels, 4 * slots), BF16),
            in_specs=[smem, vmem, vmem],
            out_specs=vmem,
            name="turn_out",
        )(counts, streams, cotangent)
        pieces = lax.all_to_all(
            turned.reshape(ctx, own, 4 * slots), CTX, 0, 0, tiled=True
        )
        marks = pieces[:, 0, 3 * slots :].astype(F32) < 2.0**50
        live = jnp.sum(marks.astype(jnp.int32), axis=1)
        order = jnp.arange(ctx, dtype=jnp.int32)
        offsets = jnp.sum(jnp.where(order[None, :] < order[:, None], live[None, :], 0), axis=1)

        taps = long_filter.T
        spectrum = mm(jnp.concatenate([taps, taps], axis=1), jnp.asarray(forward))
        first = jnp.arange(BLK)[None, :] == 0
        hre, him = spectrum[:, :BLK], spectrum[:, BLK:]
        filters = jnp.stack([hre, jnp.where(first, 0.0, him), jnp.where(first, him, hre)])
        weights = jnp.broadcast_to(
            short_filters.reshape(3 * STAP, own, 1).astype(F32), (3 * STAP, own, BLK)
        )

        padded = nb + 4
        grads, raw = pl.pallas_call(
            core_kernel,
            out_shape=(
                jax.ShapeDtypeStruct((ctx, own, 8 * BLK), BF16),
                jax.ShapeDtypeStruct((2, own, BLK), F32),
            ),
            in_specs=[smem] + [vmem] * 5,
            out_specs=(vmem, vmem),
            scratch_shapes=[
                pltpu.VMEM((4, padded, own, BLK), BF16),
                pltpu.VMEM((nb, own, BLK), F32),
                pltpu.VMEM((nb, own, BLK), F32),
                pltpu.VMEM((nb, own, BLK), BF16),
                pltpu.VMEM((nb, own, BLK), BF16),
                pltpu.VMEM((nb + 1, own, FREQ), F32),
                pltpu.VMEM((nb + 1, own, FREQ), F32),
                pltpu.VMEM((3, nb + 1, own, BLK), BF16),
                pltpu.VMEM((3, padded, own, BLK), BF16),
            ],
            compiler_params=pltpu.CompilerParams(vmem_limit_bytes=40 << 20),
            name="core",
        )(
            offsets, pieces, filters, weights, jnp.asarray(forward), jnp.asarray(backward),
        )

        squares = jnp.sum(raw * raw)
        back = lax.all_to_all(grads, CTX, 0, 0, tiled=True)
        shared = jnp.broadcast_to(squares, (1, BLK))
        for axis in ("core", "z", "x"):
            shared = jnp.sum(lax.all_gather(shared, axis, axis=0, tiled=True), axis=0, keepdims=True)
        shared, back = lax.optimization_barrier((shared, back))
        rows = lax.axis_size("y")
        shared = lax.all_to_all(jnp.broadcast_to(shared, (rows, BLK)), "y", 0, 0, tiled=True)
        stream_grads = pl.pallas_call(
            turn_back_kernel,
            out_shape=jax.ShapeDtypeStruct((3, 1, slots, channels), BF16),
            in_specs=[smem, vmem],
            out_specs=vmem,
            name="turn_back",
        )(counts, back.reshape(channels, 8 * BLK))

        rms = jnp.sqrt(jnp.sum(shared[:, 0]) / total_params + 1e-06)
        long_grad = (raw[0] / rms).T
        short_grad = (raw[1, :, : 3 * STAP] / rms).T.reshape(3, STAP, own)
        return stream_grads, long_grad, short_grad

    return jax.shard_map(
        local,
        mesh=finer,
        in_specs=(
            P(None, None, CTX, DP),
            P(None, CTX, DP),
            P(None, CTX),
            P(None, None, DP + CTX),
            P(None, DP + CTX),
        ),
        out_specs=(
            P(None, None, CTX, DP),
            P(None, DP + CTX),
            P(None, None, DP + CTX),
        ),
        check_vma=False,
    )
```

time: 157 us -> 130 us (0.83)
  waiting for transfers between devices: 58.9 us -> 36.7 us
  Pallas kernels: 40.9 us -> 26.2 us
  starting transfers between devices: 15.3 us -> 22.9 us
  blocking collectives: 32.8 us -> 34.4 us
    all_to_all x1 -> x0, blocking collectives: 32.8 us -> none  [local(): lax.all_to_all(jnp.broadcast_to(squares, (everyone, 1, BLK)), ('dp', 'ctx...]
    all_gather x0 -> x2, blocking collectives: none -> 32 us  [local(): lax.all_gather(shared, axis, axis=0, tiled=True)]
    all_to_all x2 -> x3, waiting for transfers between devices: 58.9 us -> 36.7 us  [the longest x1 33.6 us: local(): lax.all_to_all(turned.reshape(ctx, own, 4 * slots), CTX, 0, 0, tiled=True)]
    pallas_call x1, Pallas kernels: 34 us -> 19.2 us  [local(): pl.pallas_call(core_kernel, out_shape=(jax.ShapeDtypeStruct((ctx, own, 8...]
    all_to_all x2 -> x3, starting transfers between devices: 15.3 us -> 22.9 us  [the longest x1 10.3 us: local(): lax.all_to_all(turned.reshape(ctx, own, 4 * slots), CTX, 0, 0, tiled=True)]
    unnamed x0 -> x1, blocking collectives: none -> 2.45 us
    unnamed x14 -> x17, local copies, waits for them, and re-layouts: 1.01 us -> 2.71 us
  transfers between devices with their start and end apart: 2 -> 3, of which waited for: 2 -> 2; matrix products, arithmetic and copies ran while one was open for 2% -> 3% of each run, Pallas kernels for 0% -> 2%
where the time goes in v2:
time: 130 us
  waiting for transfers between devices  36.7 us (28%)
  blocking collectives  34.4 us (26%)
  Pallas kernels  26.2 us (20%)
  starting transfers between devices  22.9 us (18%)
  local copies, waits for them, and re-layouts  4.16 us (3%)
  other arithmetic  2.85 us (2%)
  between operations  2.12 us (2%)
    all_to_all x1, waiting for transfers between devices, local(): lax.all_to_all(turned.reshape(ctx, own, 4 * slots), CTX, 0, 0, tiled=True)  33.6 us
    all_gather x2, blocking collectives, local(): lax.all_gather(shared, axis, axis=0, tiled=True)  32 us
    pallas_call x1, Pallas kernels, local(): pl.pallas_call(core_kernel, out_shape=(jax.ShapeDtypeStruct((ctx, own, 8...  19.2 us
    all_to_all x1, starting transfers between devices, local(): lax.all_to_all(turned.reshape(ctx, own, 4 * slots), CTX, 0, 0, tiled=True)  10.3 us
    all_to_all x1, starting transfers between devices, local(): lax.all_to_all(jnp.broadcast_to(shared, (rows, BLK)), 'y', 0, 0, tiled=True)  7.23 us
    all_to_all x1, starting transfers between devices, local(): back = lax.all_to_all(grads, CTX, 0, 0, tiled=True)  5.41 us
    pallas_call x1, Pallas kernels, local(): pl.pallas_call(turn_out_kernel, out_shape=jax.ShapeDtypeStruct((channels,...  3.91 us
    all_to_all x1, waiting for transfers between devices, local(): lax.all_to_all(jnp.broadcast_to(shared, (rows, BLK)), 'y', 0, 0, tiled=True)  3.16 us
  transfers between devices with their start and end apart: 3, of which 2 were waited for; matrix products, arithmetic and copies ran while one was open for 3% of the time, Pallas kernels for 2%

profile of v2, /device:TPU:8, one launch (start us, length us, event | category | flops | bytes accessed | tf_op | source)
XLA Modules:
  0.0 129.7 jit_solution(7614693775059809164)
XLA Ops:
  0.6 0.0 copy-start
  1.3 3.9 %turn_out.1 = bf16[512,1280]{1,0:T(8,128)(2,1)} custom-call(s32[1,1]{1,0:T(1,128)S(6)} %copy.20.count_ref, bf16[3,1,320,512]{3,2,1,0:T(8,128)(2,1)} %s_ref.1, bf16[1,320,512]{2,1,0:T(8,128)(2,1)} %d_ref.1), custom_call_target="tpu_custom_call" | custom-call | tf_op jit(solution)/shard_map/turn_out/pallas_call | solution.py:276
  5.2 0.0 copy-start.6
  5.2 0.0 copy-start.4
  5.2 0.0 copy-start.5
  5.2 0.0 copy-start.1
  5.2 0.0 copy-start.2
  5.2 10.3 %all-to-all-start = ((bf16[32,16,1280]{2,1,0:T(8,128)(2,1)}), bf16[32,16,1280]{2,1,0:T(8,128)(2,1)S(1)}, u32[]{:S(2)}, u32[]{:S(2)}) async-start(bf16[32,16,1280]{2,1,0:T(8,128)(2,1)} %bitcast.29), calls=%async_computation | async-start | bytes 2621440 | tf_op jit(solution)/shard_map/all_to_all | solution.py:283
  15.6 0.0 copy-done.6
  15.6 0.0 copy-done
  15.6 0.0 copy-done.4
  15.6 0.1 fusion.2
  15.7 0.0 copy-done.5
  15.7 0.1 fusion
  15.9 33.6 %all-to-all-done.r_ref = bf16[32,16,1280]{2,1,0:T(8,128)(2,1)S(1)} async-done(((bf16[32,16,1280]{2,1,0:T(8,128)(2,1)}), bf16[32,16,1280]{2,1,0:T(8,128)(2,1)S(1)}, u32[]{:S(2)}, u32[]{:S(2)}) %all-to-all-start) | async-done | bytes 1310752 | tf_op jit(solution)/shard_map/all_to_all | solution.py:283
  49.5 0.8 fusion.1
  50.3 0.1 select_reduce_fusion.off_ref
  50.4 0.1 broadcast_in_dim.62.w_ref
  50.5 0.0 copy-done.1
  50.5 0.0 copy-done.2
  50.5 19.2 %core.1 = (bf16[32,16,1024]{2,1,0:T(8,128)(2,1)}, f32[2,16,128]{2,1,0:T(8,128)S(1)}) custom-call(s32[32]{0:T(128)S(1)} %select_reduce_fusion.off_ref, bf16[32,16,1280]{2,1,0:T(8,128)(2,1)S(1)} %all-to-all-done.r_ref, f32[3,16,128]{2,1,0:T(8,128)S(1)} %pad_maximum_fusion.h_ref, f32[21,16,128]{2,1,0:T(8,128)S(1)} %broadcast_in_dim.62.w_ref, ...), custom_call_target="tpu_custom_call" | custom-call | tf_op jit(solution)/shard_map/core/pallas_call | solution.py:301
  69.7 5.4 %all-to-all-start.1 = ((bf16[32,16,1024]{2,1,0:T(8,128)(2,1)}), bf16[32,16,1024]{2,1,0:T(8,128)(2,1)S(1)}, u32[]{:S(2)}, u32[]{:S(2)}) async-start(bf16[32,16,1024]{2,1,0:T(8,128)(2,1)} %get-tuple-element.8), calls=%async_computation.1 | async-start | bytes 2097152 | tf_op jit(solution)/shard_map/all_to_all | solution.py:327
  75.2 1.3 dynamic-slice
  76.4 0.6 multiply_reduce_fusion
  77.0 1.4 %dynamic-update-slice = f32[2]{0:T(128)S(1)} dynamic-update-slice(f32[2]{0:T(128)S(1)} %broadcast.17, f32[1]{0:T(128)} %bitcast.5, u32[]{:T(128)} %bitcast.6) | dynamic-update-slice | bytes 12
  78.4 2.4 %all-reduce = f32[2]{0:T(128)S(1)} all-reduce(f32[2]{0:T(128)S(1)} %dynamic-update-slice), channel_id=2, replica_groups=mesh['z'=8,'core'=2,'x'=4,'y'=8] {'core'}, use_global_device_ids=true, to_apply=%add | all-reduce | flops 2 | bytes 16
  80.9 0.1 broadcast_reduce_fusion
  81.0 22.3 %all-gather.2 = f32[8,1,128]{2,1,0:T(1,128)S(1)} all-gather(f32[1,1,128]{2,1,0:T(1,128)S(1)} %bitcast.33), channel_id=3, replica_groups=mesh['z'=8,'core'=2,'x'=4,'y'=8] {'z'}, dimensions={0}, use_global_device_ids=true | all-gather | bytes 4608 | tf_op jit(solution)/shard_map/all_gather | solution.py:330
  103.3 9.7 %all-gather.3 = f32[4,1,128]{2,1,0:T(1,128)S(1)} all-gather(f32[1,1,128]{2,1,0:T(1,128)S(1)} %bitcast.32), channel_id=4, replica_groups=mesh['z'=8,'core'=2,'x'=4,'y'=8] {'x'}, dimensions={0}, use_global_device_ids=true | all-gather | bytes 2560 | tf_op jit(solution)/shard_map/all_gather | solution.py:330
  113.0 0.0 all-to-all-done.1
  113.0 0.0 copy-start.3
  113.0 0.6 broadcast_in_dim.67
  113.7 7.2 %all-to-all-start.2 = ((f32[8,1,128]{2,1,0:T(1,128)}), f32[8,1,128]{2,1,0:T(1,128)S(1)}, u32[]{:S(2)}, u32[]{:S(2)}) async-start(f32[8,1,128]{2,1,0:T(1,128)} %broadcast_in_dim.67), calls=%async_computation.2 | async-start | bytes 8192 | tf_op jit(solution)/shard_map/all_to_all | solution.py:333
  120.9 0.0 copy-done.3
  120.9 3.0 %turn_back.1 = bf16[3,1,320,512]{3,2,1,0:T(8,128)(2,1)} custom-call(s32[1,1]{1,0:T(1,128)S(6)} %copy.20.count_ref, bf16[512,1024]{1,0:T(8,128)(2,1)} %bitcast.30), custom_call_target="tpu_custom_call" | custom-call | tf_op jit(solution)/shard_map/turn_back/pallas_call | solution.py:334
  123.9 3.2 %all-to-all-done.2 = f32[8,1,128]{2,1,0:T(1,128)S(1)} async-done(((f32[8,1,128]{2,1,0:T(1,128)}), f32[8,1,128]{2,1,0:T(1,128)S(1)}, u32[]{:S(2)}, u32[]{:S(2)}) %all-to-all-start.2) | async-done | bytes 4128 | tf_op jit(solution)/shard_map/all_to_all | solution.py:333
  127.1 0.6 slice_reduce_fusion
  128.4 0.6 divide_bitcast_fusion.1
  129.0 0.1 copy.17
  129.1 0.6 reshape.47
  (8 shorter events, 0.1 us)
Async XLA Ops:
  0.6 15.0 %copy-start = (bf16[128,16]{0,1:T(8,128)(2,1)S(1)}, bf16[128,16]{0,1:T(8,128)(2,1)}, u32[]{:S(2)}) copy-start(bf16[128,16]{0,1:T(8,128)(2,1)} %param.11) | copy-start | bytes 12292
  5.2 10.3 %copy-start.6 = (bf16[3,7,16]{2,1,0:T(8,128)(2,1)S(1)}, bf16[3,7,16]{2,1,0:T(8,128)(2,1)}, u32[]{:S(2)}) copy-start(bf16[3,7,16]{2,1,0:T(8,128)(2,1)} %param.10) | copy-start | bytes 2020
  5.2 10.4 %copy-start.4 = (bf16[128,256]{1,0:T(8,128)(2,1)S(1)}, bf16[128,256]{1,0:T(8,128)(2,1)}, u32[]{:S(2)}) copy-start(bf16[128,256]{1,0:T(8,128)(2,1)} %constant.21) | copy-start | bytes 196612
  5.2 10.5 %copy-start.5 = (bf16[128,256]{1,0:T(8,128)(2,1)S(1)}, bf16[128,256]{1,0:T(8,128)(2,1)}, u32[]{:S(2)}) copy-start(bf16[128,256]{1,0:T(8,128)(2,1)} %constant.22) | copy-start | bytes 196612
  5.2 45.3 %copy-start.1 = (bf16[768,128]{1,0:T(8,128)(2,1)S(1)}, bf16[768,128]{1,0:T(8,128)(2,1)}, u32[]{:S(2)}) copy-start(bf16[768,128]{1,0:T(8,128)(2,1)} %constant.17.clone.g_ref) | copy-start | bytes 589828
  5.2 45.3 %copy-start.2 = (bf16[256,256]{1,0:T(8,128)(2,1)S(1)}, bf16[256,256]{1,0:T(8,128)(2,1)}, u32[]{:S(2)}) copy-start(bf16[256,256]{1,0:T(8,128)(2,1)} %constant.16.clone.f_ref) | copy-start | bytes 393220
  5.2 44.2 %all-to-all-start = ((bf16[32,16,1280]{2,1,0:T(8,128)(2,1)}), bf16[32,16,1280]{2,1,0:T(8,128)(2,1)S(1)}, u32[]{:S(2)}, u32[]{:S(2)}) async-start(bf16[32,16,1280]{2,1,0:T(8,128)(2,1)} %bitcast.29), calls=%async_computation | async-start | bytes 2621440 | tf_op jit(solution)/shard_map/all_to_all | solution.py:283
  69.7 43.3 %all-to-all-start.1 = ((bf16[32,16,1024]{2,1,0:T(8,128)(2,1)}), bf16[32,16,1024]{2,1,0:T(8,128)(2,1)S(1)}, u32[]{:S(2)}, u32[]{:S(2)}) async-start(bf16[32,16,1024]{2,1,0:T(8,128)(2,1)} %get-tuple-element.8), calls=%async_computation.1 | async-start | bytes 2097152 | tf_op jit(solution)/shard_map/all_to_all | solution.py:327
  113.0 7.9 %copy-start.3 = (bf16[32,16,1024]{2,1,0:T(8,128)(2,1)}, bf16[32,16,1024]{2,1,0:T(8,128)(2,1)S(1)}, u32[]{:S(2)}) copy-start(bf16[32,16,1024]{2,1,0:T(8,128)(2,1)S(1)} %all-to-all-done.1) | copy-start | bytes 3145732
  113.7 13.4 %all-to-all-start.2 = ((f32[8,1,128]{2,1,0:T(1,128)}), f32[8,1,128]{2,1,0:T(1,128)S(1)}, u32[]{:S(2)}, u32[]{:S(2)}) async-start(f32[8,1,128]{2,1,0:T(1,128)} %broadcast_in_dim.67), calls=%async_computation.2 | async-start | bytes 8192 | tf_op jit(solution)/shard_map/all_to_all | solution.py:333

commit v3 on v2

--- a/solution.py
+++ b/solution.py
@@ -63,33 +63,45 @@
     count = count_ref[0, 0]
     wide = min(256, channels)
     eye = identity(wide)
-    for part in range(4):
-        for at in range(0, slots, 64):
-            rows = s_ref[part, 0, at : at + 64, :] if part < 3 else d_ref[0, at : at + 64, :]
-            lane = lax.broadcasted_iota(jnp.int32, (wide, 64), 1) + at
-            for c in range(0, channels, wide):
-                turned = mm_nt(eye, rows[:, c : c + wide])
-                kept = jnp.where(lane < count, turned, 0.0 if part < 3 else DEAD)
-                first = part * slots + at
-                o_ref[c : c + wide, first : first + 64] = kept.astype(BF16)
+    lane = lax.broadcasted_iota(jnp.int32, (wide, BLK), 1)
+    for first in range(0, 4 * slots, BLK):
+        pieces, token, fill = [], lane, 0.0
+        part, at = divmod(first, slots)
+        fill = DEAD if part == 3 else 0.0
+        rest = min(BLK, slots - at)
+        token = lane + at
+        for p, low, size in ((part, at, rest), (part + 1, 0, BLK - rest)):
+            if size:
+                pieces.append(s_ref[p, 0, low : low + size] if p < 3 else d_ref[0, low : low + size])
+        if rest < BLK:
+            token = jnp.where(lane < rest, token, lane - rest)
+            fill = jnp.where(lane < rest, fill, DEAD if part == 2 else 0.0)
+        rows = pieces[0] if len(pieces) == 1 else jnp.concatenate(pieces, axis=0)
+        for c in range(0, channels, wide):
+            kept = jnp.where(token < count, mm_nt(eye, rows[:, c : c + wide]), fill)
+            o_ref[c : c + wide, first : first + BLK] = kept.astype(BF16)
 
 
 def turn_back_kernel(count_ref, r_ref, o_ref):
     slots = o_ref.shape[2]
     channels = o_ref.shape[3]
     count = count_ref[0, 0]
-    eye = identity(64)
-    for part in range(3):
-        for at in range(0, slots, 64):
-            first = part * slots + at
-            turned = mm_nt(eye, r_ref[:, first : first + 64])
-            row = lax.broadcasted_iota(jnp.int32, (64, channels), 0) + at
-            o_ref[part, 0, at : at + 64, :] = jnp.where(row < count, turned, 0.0).astype(BF16)
+    eye = identity(BLK)
+    row = lax.broadcasted_iota(jnp.int32, (BLK, channels), 0)
+    for first in range(0, 3 * slots, BLK):
+        turned = mm_nt(eye, r_ref[:, first : first + BLK])
+        part, at = divmod(first, slots)
+        rest = min(BLK, slots - at)
+        kept = jnp.where(row[:rest] + at < count, turned[:rest], 0.0).astype(BF16)
+        o_ref[part, 0, at : at + rest] = kept
+        if rest < BLK and part < 2:
+            kept = jnp.where(row[: BLK - rest] < count, turned[rest:], 0.0).astype(BF16)
+            o_ref[part + 1, 0, : BLK - rest] = kept
 
 
 def core_kernel(
     off_ref, r_ref, h_ref, w_ref, f_ref, g_ref,
-    o_ref, graw_ref,
+    o_ref, graw_ref, sq_ref,
     x_ref, k_ref, v_ref, z_ref, d_ref, az_ref, ad_ref, dm_ref, out_ref,
 ):
     pieces, chans, _ = r_ref.shape
@@ -121,10 +133,11 @@
                     piece = jnp.where(lane < skip + slots - n * BLK, piece, none)
                 rolled.append(pltpu.roll(piece, turn, 1))
             early = lane < turn
+            fresh = jnp.where(early, rolled[0], rolled[1])
             x_ref[part, block] += jnp.where(early, none, rolled[0])
-            x_ref[part, block + 1] += jnp.where(early, rolled[0], rolled[1])
-            x_ref[part, block + 2] += jnp.where(early, rolled[1], rolled[2])
-            x_ref[part, block + 3] += jnp.where(early, rolled[2], none)
+            x_ref[part, block + 1] = x_ref[part, block + 1] + fresh if skip else fresh
+            x_ref[part, block + 2] = jnp.where(early, rolled[1], rolled[2])
+            x_ref[part, block + 3] = jnp.where(early, rolled[2], none)
         return carry
 
     lax.fori_loop(0, pieces, pack, 0, unroll=2)
@@ -143,23 +156,25 @@
 
     zero = jnp.zeros((chans, BLK), F32)
 
-    def features(b, carried):
-        feats, kept = [], []
-        for m in range(3):
+    for m in range(3):
+
+        def features(b, carried, m=m):
             before, here = x_ref[m, b], x_ref[m, b + 1]
             moved = [here.astype(F32)] + [later(before, here, i).astype(F32) for i in (1, 2, 3)]
             far = weighted(m, 4, moved)
-            feats.append(weighted(m, 0, moved) + later(carried[m], far, 4))
-            kept.append(far)
-        k_ref[b] = feats[1]
-        v_ref[b] = feats[2]
-        z_ref[b] = (feats[1] * feats[2]).astype(BF16)
-        d_ref[b] = (x_ref[3, b + 1].astype(F32) * feats[0]).astype(BF16)
-        return tuple(kept)
-
-    lax.fori_loop(0, nb, features, (zero,) * 3, unroll=4)
-
-    step = 16
+            feature = weighted(m, 0, moved) + later(carried, far, 4)
+            if m == 0:
+                d_ref[b] = (x_ref[3, b + 1].astype(F32) * feature).astype(BF16)
+            elif m == 1:
+                k_ref[b] = feature
+            else:
+                v_ref[b] = feature
+                z_ref[b] = (k_ref[b] * feature).astype(BF16)
+            return far
+
+        lax.fori_loop(0, nb, features, zero, unroll=8)
+
+    step = 32
     az_ref[0] = jnp.zeros((chans, FREQ), F32)
     ad_ref[nb] = jnp.zeros((chans, FREQ), F32)
 
@@ -178,7 +193,7 @@
     sign = 1.0 - 2.0 * lax.bitwise_and(
         lax.broadcasted_iota(jnp.int32, (1, 1, FREQ), 2), 1
     ).astype(F32)
-    chunk = 8
+    chunk = 16
 
     def turn(re, im):
         rehi, relo = split2(re.reshape(-1, BLK))
@@ -209,7 +224,8 @@
     p1, p2, p3 = lax.fori_loop(0, nb // chunk, long, (zero, zero, zero))
     lre = p1 + jnp.where(lane == 0, 0.0, p2)
     lim = jnp.where(lane == 0, p2, p3)
-    graw_ref[0] = turn(lre[None], lim[None])[0]
+    longs = turn(lre[None], lim[None])[0]
+    graw_ref[0] = longs
 
     dm_ref[:, nb] = jnp.zeros((3, chans, BLK), BF16)
     out_ref[:, 0] = jnp.zeros((3, chans, BLK), BF16)
@@ -231,11 +247,13 @@
             fresh += [sums[4 + i] + old * moved[i] for i in range(3)]
             return tuple(fresh), far
 
-        sums, _ = lax.fori_loop(0, nb, back, ((zero,) * STAP, zero), unroll=4)
+        sums, _ = lax.fori_loop(0, nb, back, ((zero,) * STAP, zero), unroll=8)
         for i in range(STAP):
             column = jnp.sum(sums[i], axis=1, keepdims=True)
             shorts = jnp.where(lane == m * STAP + i, column, shorts)
     graw_ref[1] = shorts
+    squares = jnp.sum(longs * longs + shorts * shorts, axis=0, keepdims=True)
+    sq_ref[...] = jnp.broadcast_to(jnp.sum(squares, axis=1, keepdims=True), (1, BLK))
 
     def unpack(j, carry):
         offset = off_ref[j]
@@ -298,14 +316,15 @@
         )
 
         padded = nb + 4
-        grads, raw = pl.pallas_call(
+        grads, raw, shared = pl.pallas_call(
             core_kernel,
             out_shape=(
                 jax.ShapeDtypeStruct((ctx, own, 8 * BLK), BF16),
                 jax.ShapeDtypeStruct((2, own, BLK), F32),
+                jax.ShapeDtypeStruct((1, BLK), F32),
             ),
             in_specs=[smem] + [vmem] * 5,
-            out_specs=(vmem, vmem),
+            out_specs=(vmem, vmem, vmem),
             scratch_shapes=[
                 pltpu.VMEM((4, padded, own, BLK), BF16),
                 pltpu.VMEM((nb, own, BLK), F32),
@@ -323,10 +342,8 @@
             offsets, pieces, filters, weights, jnp.asarray(forward), jnp.asarray(backward),
         )
 
-        squares = jnp.sum(raw * raw)
         back = lax.all_to_all(grads, CTX, 0, 0, tiled=True)
-        shared = jnp.broadcast_to(squares, (1, BLK))
-        for axis in ("core", "z", "x"):
+        for axis in (DP, "x"):
             shared = jnp.sum(lax.all_gather(shared, axis, axis=0, tiled=True), axis=0, keepdims=True)
         shared, back = lax.optimization_barrier((shared, back))
         rows = lax.axis_size("y")

time: 130 us -> 121 us (0.931)
  Pallas kernels: 26.2 us -> 21.9 us
  local copies, waits for them, and re-layouts: 4.16 us -> 1.49 us
  blocking collectives: 34.4 us -> 32.9 us
    pallas_call x1, Pallas kernels: 19.2 us -> 16.1 us  [local(): pl.pallas_call(core_kernel, out_shape=(jax.ShapeDtypeStruct((ctx, own, 8...]
    unnamed x17 -> x14, local copies, waits for them, and re-layouts: 2.71 us -> 0.03 us
    unnamed x1 -> x0, blocking collectives: 2.45 us -> none
  transfers between devices with their start and end apart: 3 -> 3, of which waited for: 2 -> 2; matrix products, arithmetic and copies ran while one was open for 3% -> 0% of each run, Pallas kernels for 2% -> 2%
where the time goes in v3:
time: 121 us
  waiting for transfers between devices  37.2 us (31%)
  blocking collectives  32.9 us (27%)
  starting transfers between devices  22.9 us (19%)
  Pallas kernels  21.9 us (18%)
  other arithmetic  2.17 us (2%)
  between operations  2.11 us (2%)
  local copies, waits for them, and re-layouts  1.49 us (1%)
    all_to_all x1, waiting for transfers between devices, local(): lax.all_to_all(turned.reshape(ctx, own, 4 * slots), CTX, 0, 0, tiled=True)  33.6 us
    all_gather x2, blocking collectives, local(): lax.all_gather(shared, axis, axis=0, tiled=True)  32.9 us
    pallas_call x1, Pallas kernels, local(): pl.pallas_call(core_kernel, out_shape=(jax.ShapeDtypeStruct((ctx, own, 8...  16.1 us
    all_to_all x1, starting transfers between devices, local(): lax.all_to_all(turned.reshape(ctx, own, 4 * slots), CTX, 0, 0, tiled=True)  10.3 us
    all_to_all x1, starting transfers between devices, local(): lax.all_to_all(jnp.broadcast_to(shared, (rows, BLK)), 'y', 0, 0, tiled=True)  7.23 us
    all_to_all x1, starting transfers between devices, local(): back = lax.all_to_all(grads, CTX, 0, 0, tiled=True)  5.4 us
    all_to_all x1, waiting for transfers between devices, local(): lax.all_to_all(jnp.broadcast_to(shared, (rows, BLK)), 'y', 0, 0, tiled=True)  3.58 us
    pallas_call x1, Pallas kernels, local(): pl.pallas_call(turn_out_kernel, out_shape=jax.ShapeDtypeStruct((channels,...  3.19 us
  transfers between devices with their start and end apart: 3, of which 2 were waited for; matrix products, arithmetic and copies ran while one was open for 0% of the time, Pallas kernels for 2%

profile of v3, /device:TPU:8, one launch (start us, length us, event | category | flops | bytes accessed | tf_op | source)
XLA Modules:
  0.0 120.9 jit_solution(12134602355687673899)
XLA Ops:
  0.6 0.0 copy-start
  1.3 3.2 %turn_out.1 = bf16[512,1280]{1,0:T(8,128)(2,1)} custom-call(s32[1,1]{1,0:T(1,128)S(6)} %copy.19.count_ref, bf16[3,1,320,512]{3,2,1,0:T(8,128)(2,1)} %s_ref.1, bf16[1,320,512]{2,1,0:T(8,128)(2,1)} %d_ref.1), custom_call_target="tpu_custom_call" | custom-call | tf_op jit(solution)/shard_map/turn_out/pallas_call | solution.py:294
  4.5 0.0 copy-start.6
  4.5 0.0 copy-start.4
  4.5 0.0 copy-start.5
  4.5 0.0 copy-start.1
  4.5 0.0 copy-start.2
  4.5 10.3 %all-to-all-start = ((bf16[32,16,1280]{2,1,0:T(8,128)(2,1)}), bf16[32,16,1280]{2,1,0:T(8,128)(2,1)S(1)}, u32[]{:S(2)}, u32[]{:S(2)}) async-start(bf16[32,16,1280]{2,1,0:T(8,128)(2,1)} %bitcast.28), calls=%async_computation | async-start | bytes 2621440 | tf_op jit(solution)/shard_map/all_to_all | solution.py:301
  14.8 0.0 copy-done.6
  14.9 0.0 copy-done
  14.9 0.0 copy-done.4
  14.9 0.1 fusion.2
  15.0 0.0 copy-done.5
  15.0 0.1 fusion
  15.2 33.6 %all-to-all-done.r_ref = bf16[32,16,1280]{2,1,0:T(8,128)(2,1)S(1)} async-done(((bf16[32,16,1280]{2,1,0:T(8,128)(2,1)}), bf16[32,16,1280]{2,1,0:T(8,128)(2,1)S(1)}, u32[]{:S(2)}, u32[]{:S(2)}) %all-to-all-start) | async-done | bytes 1310752 | tf_op jit(solution)/shard_map/all_to_all | solution.py:301
  48.8 0.8 fusion.1
  49.5 0.1 select_reduce_fusion.off_ref
  49.6 0.1 broadcast_in_dim.56.w_ref
  49.8 0.0 copy-done.1
  49.8 0.0 copy-done.2
  49.8 16.1 %core.1 = (bf16[32,16,1024]{2,1,0:T(8,128)(2,1)}, f32[2,16,128]{2,1,0:T(8,128)S(1)}, f32[1,128]{1,0:T(1,128)S(1)}) custom-call(s32[32]{0:T(128)S(1)} %select_reduce_fusion.off_ref, bf16[32,16,1280]{2,1,0:T(8,128)(2,1)S(1)} %all-to-all-done.r_ref, f32[3,16,128]{2,1,0:T(8,128)S(1)} %pad_maximum_fusion.h_ref, f32[21,16,128]{2,1,0:T(8,128)S(1)} %broadcast_in_dim.56.w_ref, ...), custom_call_target="tpu_custom_call" | custom-call | tf_op jit(solution)/shard_map/core/pallas_call | solution.py:319
  65.9 5.4 %all-to-all-start.1 = ((bf16[32,16,1024]{2,1,0:T(8,128)(2,1)}), bf16[32,16,1024]{2,1,0:T(8,128)(2,1)S(1)}, u32[]{:S(2)}, u32[]{:S(2)}) async-start(bf16[32,16,1024]{2,1,0:T(8,128)(2,1)} %get-tuple-element.9), calls=%async_computation.1 | async-start | bytes 2097152 | tf_op jit(solution)/shard_map/all_to_all | solution.py:345
  71.3 23.2 %all-gather.1 = f32[16,1,128]{2,1,0:T(1,128)S(1)} all-gather(f32[1,1,128]{2,1,0:T(1,128)S(1)} %bitcast.27), channel_id=1, replica_groups=mesh['z'=8,'core'=2,'x'=4,'y'=8] {'z','core'}, dimensions={0}, use_global_device_ids=true | all-gather | bytes 8704 | tf_op jit(solution)/shard_map/all_gather | solution.py:347
  94.5 9.7 %all-gather.2 = f32[4,1,128]{2,1,0:T(1,128)S(1)} all-gather(f32[1,1,128]{2,1,0:T(1,128)S(1)} %bitcast.31), channel_id=2, replica_groups=mesh['z'=8,'core'=2,'x'=4,'y'=8] {'x'}, dimensions={0}, use_global_device_ids=true | all-gather | bytes 2560 | tf_op jit(solution)/shard_map/all_gather | solution.py:347
  104.2 0.0 all-to-all-done.1
  104.2 0.0 copy-start.3
  104.2 0.6 broadcast_in_dim.59
  104.9 7.2 %all-to-all-start.2 = ((f32[8,1,128]{2,1,0:T(1,128)}), f32[8,1,128]{2,1,0:T(1,128)S(1)}, u32[]{:S(2)}, u32[]{:S(2)}) async-start(f32[8,1,128]{2,1,0:T(1,128)} %broadcast_in_dim.59), calls=%async_computation.2 | async-start | bytes 8192 | tf_op jit(solution)/shard_map/all_to_all | solution.py:350
  112.1 0.0 copy-done.3
  112.1 2.6 %turn_back.1 = bf16[3,1,320,512]{3,2,1,0:T(8,128)(2,1)} custom-call(s32[1,1]{1,0:T(1,128)S(6)} %copy.19.count_ref, bf16[512,1024]{1,0:T(8,128)(2,1)} %bitcast.29), custom_call_target="tpu_custom_call" | custom-call | tf_op jit(solution)/shard_map/turn_back/pallas_call | solution.py:351
  114.7 3.6 %all-to-all-done.2 = f32[8,1,128]{2,1,0:T(1,128)S(1)} async-done(((f32[8,1,128]{2,1,0:T(1,128)}), f32[8,1,128]{2,1,0:T(1,128)S(1)}, u32[]{:S(2)}, u32[]{:S(2)}) %all-to-all-start.2) | async-done | bytes 4128 | tf_op jit(solution)/shard_map/all_to_all | solution.py:350
  118.3 0.6 slice_reduce_fusion
  119.6 0.6 divide_bitcast_fusion.1
  120.2 0.1 copy.17
  120.3 0.6 reshape.47
  (7 shorter events, 0.1 us)
Async XLA Ops:
  0.6 14.2 %copy-start = (bf16[128,16]{0,1:T(8,128)(2,1)S(1)}, bf16[128,16]{0,1:T(8,128)(2,1)}, u32[]{:S(2)}) copy-start(bf16[128,16]{0,1:T(8,128)(2,1)} %param.11) | copy-start | bytes 12292
  4.5 10.3 %copy-start.6 = (bf16[3,7,16]{2,1,0:T(8,128)(2,1)S(1)}, bf16[3,7,16]{2,1,0:T(8,128)(2,1)}, u32[]{:S(2)}) copy-start(bf16[3,7,16]{2,1,0:T(8,128)(2,1)} %param.10) | copy-start | bytes 2020
  4.5 10.4 %copy-start.4 = (bf16[128,256]{1,0:T(8,128)(2,1)S(1)}, bf16[128,256]{1,0:T(8,128)(2,1)}, u32[]{:S(2)}) copy-start(bf16[128,256]{1,0:T(8,128)(2,1)} %constant.21) | copy-start | bytes 196612
  4.5 10.5 %copy-start.5 = (bf16[128,256]{1,0:T(8,128)(2,1)S(1)}, bf16[128,256]{1,0:T(8,128)(2,1)}, u32[]{:S(2)}) copy-start(bf16[128,256]{1,0:T(8,128)(2,1)} %constant.22) | copy-start | bytes 196612
  4.5 45.3 %copy-start.1 = (bf16[768,128]{1,0:T(8,128)(2,1)S(1)}, bf16[768,128]{1,0:T(8,128)(2,1)}, u32[]{:S(2)}) copy-start(bf16[768,128]{1,0:T(8,128)(2,1)} %constant.17.clone.g_ref) | copy-start | bytes 589828
  4.5 45.3 %copy-start.2 = (bf16[256,256]{1,0:T(8,128)(2,1)S(1)}, bf16[256,256]{1,0:T(8,128)(2,1)}, u32[]{:S(2)}) copy-start(bf16[256,256]{1,0:T(8,128)(2,1)} %constant.16.clone.f_ref) | copy-start | bytes 393220
  4.5 44.2 %all-to-all-start = ((bf16[32,16,1280]{2,1,0:T(8,128)(2,1)}), bf16[32,16,1280]{2,1,0:T(8,128)(2,1)S(1)}, u32[]{:S(2)}, u32[]{:S(2)}) async-start(bf16[32,16,1280]{2,1,0:T(8,128)(2,1)} %bitcast.28), calls=%async_computation | async-start | bytes 2621440 | tf_op jit(solution)/shard_map/all_to_all | solution.py:301
  65.9 38.3 %all-to-all-start.1 = ((bf16[32,16,1024]{2,1,0:T(8,128)(2,1)}), bf16[32,16,1024]{2,1,0:T(8,128)(2,1)S(1)}, u32[]{:S(2)}, u32[]{:S(2)}) async-start(bf16[32,16,1024]{2,1,0:T(8,128)(2,1)} %get-tuple-element.9), calls=%async_computation.1 | async-start | bytes 2097152 | tf_op jit(solution)/shard_map/all_to_all | solution.py:345
  104.2 7.9 %copy-start.3 = (bf16[32,16,1024]{2,1,0:T(8,128)(2,1)}, bf16[32,16,1024]{2,1,0:T(8,128)(2,1)S(1)}, u32[]{:S(2)}) copy-start(bf16[32,16,1024]{2,1,0:T(8,128)(2,1)S(1)} %all-to-all-done.1) | copy-start | bytes 3145732
  104.9 13.4 %all-to-all-start.2 = ((f32[8,1,128]{2,1,0:T(1,128)}), f32[8,1,128]{2,1,0:T(1,128)S(1)}, u32[]{:S(2)}, u32[]{:S(2)}) async-start(f32[8,1,128]{2,1,0:T(1,128)} %broadcast_in_dim.59), calls=%async_computation.2 | async-start | bytes 8192 | tf_op jit(solution)/shard_map/all_to_all | solution.py:350

commit v4 on v3

--- a/solution.py
+++ b/solution.py
@@ -36,6 +36,14 @@
     weight[0] = weight[BLK] = 1.0 / FREQ
     backward = forward.T * weight
     return split_np(forward), split_np(backward)
+
+
+def shift_tables():
+    row = np.arange(FREQ)[:, None]
+    col = np.arange(BLK)[None, :]
+    past = [row == BLK + col - i for i in range(1, STAP)]
+    future = [row == col + i for i in range(1, STAP)]
+    return tuple(np.concatenate(t, axis=1).astype(jnp.bfloat16) for t in (past, future))
 
 
 def split2(x):
@@ -100,9 +108,9 @@
 
 
 def core_kernel(
-    off_ref, r_ref, h_ref, w_ref, f_ref, g_ref,
+    off_ref, r_ref, h_ref, w_ref, f_ref, g_ref, fs_ref, bs_ref,
     o_ref, graw_ref, sq_ref,
-    x_ref, k_ref, v_ref, z_ref, d_ref, az_ref, ad_ref, dm_ref, out_ref,
+    xq_ref, xk_ref, xv_ref, xd_ref, k_ref, v_ref, z_ref, d_ref, az_ref, ad_ref, dm_ref, out_ref, sum_ref,
 ):
     pieces, chans, _ = r_ref.shape
     slots = r_ref.shape[2] // 4
@@ -110,7 +118,9 @@
     lane = lax.broadcasted_iota(jnp.int32, (chans, BLK), 1)
 
     none = jnp.zeros((chans, BLK), BF16)
-    x_ref[...] = jnp.zeros(x_ref.shape, BF16)
+    x_refs = (xq_ref, xk_ref, xv_ref, xd_ref)
+    for ref in x_refs:
+        ref[...] = jnp.zeros(ref.shape, BF16)
 
     def place(offset, part):
         aligned = part * slots // BLK * BLK
@@ -134,45 +144,42 @@
                 rolled.append(pltpu.roll(piece, turn, 1))
             early = lane < turn
             fresh = jnp.where(early, rolled[0], rolled[1])
-            x_ref[part, block] += jnp.where(early, none, rolled[0])
-            x_ref[part, block + 1] = x_ref[part, block + 1] + fresh if skip else fresh
-            x_ref[part, block + 2] = jnp.where(early, rolled[1], rolled[2])
-            x_ref[part, block + 3] = jnp.where(early, rolled[2], none)
+            x_ref = x_refs[part]
+            x_ref[block] += jnp.where(early, none, rolled[0])
+            x_ref[block + 1] = x_ref[block + 1] + fresh if skip else fresh
+            x_ref[block + 2] = jnp.where(early, rolled[1], rolled[2])
+            x_ref[block + 3] = jnp.where(early, rolled[2], none)
         return carry
 
     lax.fori_loop(0, pieces, pack, 0, unroll=2)
 
-    def later(before, here, i):
-        return pltpu.roll(jnp.where(lane >= BLK - i, before, here), i, 1)
-
-    def sooner(here, after, i):
-        return pltpu.roll(jnp.where(lane < i, after, here), BLK - i, 1)
-
-    def weighted(m, first, moved):
-        total = w_ref[m * STAP + first] * moved[0]
-        for i in range(1, min(len(moved), STAP - first)):
-            total = total + w_ref[m * STAP + first + i] * moved[i]
-        return total
-
     zero = jnp.zeros((chans, BLK), F32)
-
-    for m in range(3):
-
-        def features(b, carried, m=m):
-            before, here = x_ref[m, b], x_ref[m, b + 1]
-            moved = [here.astype(F32)] + [later(before, here, i).astype(F32) for i in (1, 2, 3)]
-            far = weighted(m, 4, moved)
-            feature = weighted(m, 0, moved) + later(carried, far, 4)
-            if m == 0:
-                d_ref[b] = (x_ref[3, b + 1].astype(F32) * feature).astype(BF16)
-            elif m == 1:
-                k_ref[b] = feature
-            else:
-                v_ref[b] = feature
-                z_ref[b] = (k_ref[b] * feature).astype(BF16)
-            return far
-
-        lax.fori_loop(0, nb, features, zero, unroll=8)
+    group = 32
+
+    def moved_blocks(first, second, table_ref):
+        pairs = jnp.concatenate([first.reshape(-1, BLK), second.reshape(-1, BLK)], axis=1)
+        for at in range(0, (STAP - 1) * BLK, FREQ):
+            both = mm(pairs, table_ref[:, at : at + FREQ])
+            yield both[:, :BLK].reshape(-1, chans, BLK)
+            yield both[:, BLK:].reshape(-1, chans, BLK)
+
+    def features(c, carry):
+        at = c * group
+        before = jnp.concatenate([x_refs[m][pl.ds(at, group)] for m in range(3)])
+        here = jnp.concatenate([x_refs[m][pl.ds(at + 1, group)] for m in range(3)])
+        feats = [
+            w_ref[m * STAP][None] * here[m * group : (m + 1) * group].astype(F32) for m in range(3)
+        ]
+        for i, moved in enumerate(moved_blocks(before, here, fs_ref), 1):
+            for m in range(3):
+                feats[m] += w_ref[m * STAP + i][None] * moved[m * group : (m + 1) * group]
+        k_ref[pl.ds(at, group)] = feats[1]
+        v_ref[pl.ds(at, group)] = feats[2]
+        z_ref[pl.ds(at, group)] = (feats[1] * feats[2]).astype(BF16)
+        d_ref[pl.ds(at, group)] = (xd_ref[pl.ds(at + 1, group)].astype(F32) * feats[0]).astype(BF16)
+        return carry
+
+    lax.fori_loop(0, nb // group, features, 0)
 
     step = 32
     az_ref[0] = jnp.zeros((chans, FREQ), F32)
@@ -193,7 +200,7 @@
     sign = 1.0 - 2.0 * lax.bitwise_and(
         lax.broadcasted_iota(jnp.int32, (1, 1, FREQ), 2), 1
     ).astype(F32)
-    chunk = 16
+    chunk = 32
 
     def turn(re, im):
         rehi, relo = split2(re.reshape(-1, BLK))
@@ -212,11 +219,14 @@
         p1 = p1 + jnp.sum(ore * zre, axis=0)
         p2 = p2 + jnp.sum(oim * zim, axis=0)
         p3 = p3 + jnp.sum(oim * zre - ore * zim, axis=0)
-        y = turn(zre * hre - zim * him, zim * hny + zre * him)
-        dm_ref[0, pl.ds(at, chunk)] = (x_ref[3, pl.ds(at + 1, chunk)].astype(F32) * y).astype(BF16)
         both = own + sign * ad_ref[pl.ds(at + 1, chunk)]
         dre, dim = both[:, :, :BLK], both[:, :, BLK:]
-        dz = turn(dre * hre + dim * him, dim * hny - dre * him)
+        turned = turn(
+            jnp.concatenate([zre * hre - zim * him, dre * hre + dim * him]),
+            jnp.concatenate([zim * hny + zre * him, dim * hny - dre * him]),
+        )
+        y, dz = turned[:chunk], turned[chunk:]
+        dm_ref[0, pl.ds(at, chunk)] = (xd_ref[pl.ds(at + 1, chunk)].astype(F32) * y).astype(BF16)
         dm_ref[1, pl.ds(at, chunk)] = (dz * v_ref[pl.ds(at, chunk)]).astype(BF16)
         dm_ref[2, pl.ds(at, chunk)] = (dz * k_ref[pl.ds(at, chunk)]).astype(BF16)
         return p1, p2, p3
@@ -231,26 +241,33 @@
     out_ref[:, 0] = jnp.zeros((3, chans, BLK), BF16)
     for extra in range(nb + 1, out_ref.shape[1]):
         out_ref[:, extra] = jnp.zeros((3, chans, BLK), BF16)
+    sum_ref[...] = jnp.zeros(sum_ref.shape, F32)
+
+    def back(c, carry):
+        at = c * group
+        here = dm_ref[:, pl.ds(at, group)].reshape(3 * group, chans, BLK)
+        after = dm_ref[:, pl.ds(at + 1, group)].reshape(3 * group, chans, BLK)
+        totals = [0.0] * 3
+
+        def tap(i, moved):
+            for m in range(3):
+                stream = x_refs[m][pl.ds(at + 1, group)].astype(F32)
+                part = moved[m * group : (m + 1) * group]
+                totals[m] += w_ref[m * STAP + i][None] * part
+                sum_ref[m * STAP + i] += jnp.sum(stream * part, axis=0)
+
+        tap(0, here.astype(F32))
+        for i, moved in enumerate(moved_blocks(here, after, bs_ref), 1):
+            tap(i, moved)
+        for m in range(3):
+            out_ref[m, pl.ds(at + 1, group)] = totals[m].astype(BF16)
+        return carry
+
+    lax.fori_loop(0, nb // group, back, 0)
     shorts = zero
-    for m in range(3):
-
-        def back(n, carried, m=m):
-            sums, far_after = carried
-            b = nb - 1 - n
-            here, after, stream = dm_ref[m, b], dm_ref[m, b + 1], x_ref[m, b + 1]
-            old = later(x_ref[m, b], stream, 4).astype(F32)
-            stream = stream.astype(F32)
-            moved = [here.astype(F32)] + [sooner(here, after, i).astype(F32) for i in (1, 2, 3)]
-            far = weighted(m, 4, moved)
-            out_ref[m, b + 1] = (weighted(m, 0, moved) + sooner(far, far_after, 4)).astype(BF16)
-            fresh = [sums[i] + stream * moved[i] for i in range(4)]
-            fresh += [sums[4 + i] + old * moved[i] for i in range(3)]
-            return tuple(fresh), far
-
-        sums, _ = lax.fori_loop(0, nb, back, ((zero,) * STAP, zero), unroll=8)
-        for i in range(STAP):
-            column = jnp.sum(sums[i], axis=1, keepdims=True)
-            shorts = jnp.where(lane == m * STAP + i, column, shorts)
+    for i in range(3 * STAP):
+        column = jnp.sum(sum_ref[i], axis=1, keepdims=True)
+        shorts = jnp.where(lane == i, column, shorts)
     graw_ref[1] = shorts
     squares = jnp.sum(longs * longs + shorts * shorts, axis=0, keepdims=True)
     sq_ref[...] = jnp.broadcast_to(jnp.sum(squares, axis=1, keepdims=True), (1, BLK))
@@ -279,6 +296,7 @@
     cores = min(2, mesh.shape["dp"])
     finer = Mesh(mesh.devices.reshape(-1, cores, 4, ctx // 4), ("z", "core", "x", "y"))
     (fh, fl), (gh, gl) = dft_tables()
+    past, future = shift_tables()
     forward = np.concatenate([fh, fl])
     backward = np.concatenate([gh, gh, gl])
     smem = pl.BlockSpec(memory_space=pltpu.SMEM)
@@ -323,10 +341,13 @@
                 jax.ShapeDtypeStruct((2, own, BLK), F32),
                 jax.ShapeDtypeStruct((1, BLK), F32),
             ),
-            in_specs=[smem] + [vmem] * 5,
+            in_specs=[smem] + [vmem] * 7,
             out_specs=(vmem, vmem, vmem),
             scratch_shapes=[
-                pltpu.VMEM((4, padded, own, BLK), BF16),
+                pltpu.VMEM((padded, own, BLK), BF16),
+                pltpu.VMEM((padded, own, BLK), BF16),
+                pltpu.VMEM((padded, own, BLK), BF16),
+                pltpu.VMEM((padded, own, BLK), BF16),
                 pltpu.VMEM((nb, own, BLK), F32),
                 pltpu.VMEM((nb, own, BLK), F32),
                 pltpu.VMEM((nb, own, BLK), BF16),
@@ -335,19 +356,22 @@
                 pltpu.VMEM((nb + 1, own, FREQ), F32),
                 pltpu.VMEM((3, nb + 1, own, BLK), BF16),
                 pltpu.VMEM((3, padded, own, BLK), BF16),
+                pltpu.VMEM((3 * STAP, own, BLK), F32),
             ],
             compiler_params=pltpu.CompilerParams(vmem_limit_bytes=40 << 20),
             name="core",
         )(
             offsets, pieces, filters, weights, jnp.asarray(forward), jnp.asarray(backward),
+            jnp.asarray(past), jnp.asarray(future),
         )
 
         back = lax.all_to_all(grads, CTX, 0, 0, tiled=True)
         for axis in (DP, "x"):
             shared = jnp.sum(lax.all_gather(shared, axis, axis=0, tiled=True), axis=0, keepdims=True)
-        shared, back = lax.optimization_barrier((shared, back))
-        rows = lax.axis_size("y")
-        shared = lax.all_to_all(jnp.broadcast_to(shared, (rows, BLK)), "y", 0, 0, tiled=True)
+        shared = jnp.broadcast_to(shared, (lax.axis_size("y"), BLK))
+        short_raw = raw[1, :, : 3 * STAP].T.reshape(3, STAP, own)
+        shared, back, short_raw = lax.optimization_barrier((shared, back, short_raw))
+        shared = lax.all_to_all(shared, "y", 0, 0, tiled=True)
         stream_grads = pl.pallas_call(
             turn_back_kernel,
             out_shape=jax.ShapeDtypeStruct((3, 1, slots, channels), BF16),
@@ -358,7 +382,7 @@
 
         rms = jnp.sqrt(jnp.sum(shared[:, 0]) / total_params + 1e-06)
         long_grad = (raw[0] / rms).T
-        short_grad = (raw[1, :, : 3 * STAP] / rms).T.reshape(3, STAP, own)
+        short_grad = short_raw / rms
         return stream_grads, long_grad, short_grad
 
     return jax.shard_map(

time: 121 us -> 116 us (0.959)
  Pallas kernels: 21.9 us -> 16.1 us
    pallas_call x1, Pallas kernels: 16.1 us -> 10.4 us  [local(): pl.pallas_call(core_kernel, out_shape=(jax.ShapeDtypeStruct((ctx, own, 8...]
where the time goes in v4:
time: 116 us; the launch traced here: 115 us
  waiting for transfers between devices  37.2 us (32%)
  blocking collectives  32.8 us (28%)
  starting transfers between devices  22.9 us (20%)
  Pallas kernels  16.1 us (14%)
  other arithmetic  2.78 us (2%)
  between operations  2.14 us (2%)
    all_to_all x1, waiting for transfers between devices, local(): lax.all_to_all(turned.reshape(ctx, own, 4 * slots), CTX, 0, 0, tiled=True)  33.6 us
    all_gather x2, blocking collectives, local(): lax.all_gather(shared, axis, axis=0, tiled=True)  32.8 us
    pallas_call x1, Pallas kernels, local(): pl.pallas_call(core_kernel, out_shape=(jax.ShapeDtypeStruct((ctx, own, 8...  10.4 us
    all_to_all x1, starting transfers between devices, local(): lax.all_to_all(turned.reshape(ctx, own, 4 * slots), CTX, 0, 0, tiled=True)  10.3 us
    all_to_all x1, starting transfers between devices, local(): shared = lax.all_to_all(shared, 'y', 0, 0, tiled=True)  7.23 us
    all_to_all x1, starting transfers between devices, local(): back = lax.all_to_all(grads, CTX, 0, 0, tiled=True)  5.41 us
    all_to_all x1, waiting for transfers between devices, local(): shared = lax.all_to_all(shared, 'y', 0, 0, tiled=True)  3.58 us
    pallas_call x1, Pallas kernels, local(): pl.pallas_call(turn_out_kernel, out_shape=jax.ShapeDtypeStruct((channels,...  3.17 us
  transfers between devices with their start and end apart: 3, of which 2 were waited for; matrix products, arithmetic and copies ran while one was open for 0% of the time, Pallas kernels for 2%

profile of v4, /device:TPU:8, one launch (start us, length us, event | category | flops | bytes accessed | tf_op | source)
XLA Modules:
  0.0 115.1 jit_solution(58906237734128581)
XLA Ops:
  0.6 0.0 copy-start
  1.3 3.2 %turn_out.1 = bf16[512,1280]{1,0:T(8,128)(2,1)} custom-call(s32[1,1]{1,0:T(1,128)S(6)} %copy.17.count_ref, bf16[3,1,320,512]{3,2,1,0:T(8,128)(2,1)} %s_ref.1, bf16[1,320,512]{2,1,0:T(8,128)(2,1)} %d_ref.1), custom_call_target="tpu_custom_call" | custom-call | tf_op jit(solution)/shard_map/turn_out/pallas_call | solution.py:312
  4.5 0.0 copy-start.8
  4.5 0.0 copy-start.6
  4.5 0.0 copy-start.7
  4.5 0.0 copy-start.1
  4.5 0.0 copy-start.2
  4.5 0.0 copy-start.3
  4.5 0.0 copy-start.4
  4.5 10.3 %all-to-all-start = ((bf16[32,16,1280]{2,1,0:T(8,128)(2,1)}), bf16[32,16,1280]{2,1,0:T(8,128)(2,1)S(1)}, u32[]{:S(2)}, u32[]{:S(2)}) async-start(bf16[32,16,1280]{2,1,0:T(8,128)(2,1)} %bitcast.27), calls=%async_computation | async-start | bytes 2621440 | tf_op jit(solution)/shard_map/all_to_all | solution.py:319
  14.8 0.0 copy-done.8
  14.9 0.0 copy-done
  14.9 0.0 copy-done.6
  14.9 0.1 fusion.2
  15.0 0.0 copy-done.7
  15.0 0.1 fusion
  15.2 33.6 %all-to-all-done.r_ref = bf16[32,16,1280]{2,1,0:T(8,128)(2,1)S(1)} async-done(((bf16[32,16,1280]{2,1,0:T(8,128)(2,1)}), bf16[32,16,1280]{2,1,0:T(8,128)(2,1)S(1)}, u32[]{:S(2)}, u32[]{:S(2)}) %all-to-all-start) | async-done | bytes 1310752 | tf_op jit(solution)/shard_map/all_to_all | solution.py:319
  48.8 0.8 fusion.1
  49.5 0.1 select_reduce_fusion.off_ref
  49.7 0.1 broadcast_in_dim.54.w_ref
  49.8 0.0 copy-done.1
  49.8 0.0 copy-done.2
  49.8 0.0 copy-done.3
  49.8 0.0 copy-done.4
  49.8 10.4 %core.1 = (bf16[32,16,1024]{2,1,0:T(8,128)(2,1)}, f32[2,16,128]{2,1,0:T(8,128)S(1)}, f32[1,128]{1,0:T(1,128)S(1)}) custom-call(s32[32]{0:T(128)S(1)} %select_reduce_fusion.off_ref, bf16[32,16,1280]{2,1,0:T(8,128)(2,1)S(1)} %all-to-all-done.r_ref, f32[3,16,128]{2,1,0:T(8,128)S(1)} %pad_maximum_fusion.h_ref, f32[21,16,128]{2,1,0:T(8,128)S(1)} %broadcast_in_dim.54.w_ref, ...), custom_call_target="tpu_custom_call" | custom-call | tf_op jit(solution)/shard_map/core/pallas_call | solution.py:337
  60.2 5.4 %all-to-all-start.1 = ((bf16[32,16,1024]{2,1,0:T(8,128)(2,1)}), bf16[32,16,1024]{2,1,0:T(8,128)(2,1)S(1)}, u32[]{:S(2)}, u32[]{:S(2)}) async-start(bf16[32,16,1024]{2,1,0:T(8,128)(2,1)} %get-tuple-element.10), calls=%async_computation.1 | async-start | bytes 2097152 | tf_op jit(solution)/shard_map/all_to_all | solution.py:368
  65.6 23.2 %all-gather.1 = f32[16,1,128]{2,1,0:T(1,128)S(1)} all-gather(f32[1,1,128]{2,1,0:T(1,128)S(1)} %bitcast.26), channel_id=1, replica_groups=mesh['z'=8,'core'=2,'x'=4,'y'=8] {'z','core'}, dimensions={0}, use_global_device_ids=true | all-gather | bytes 8704 | tf_op jit(solution)/shard_map/all_gather | solution.py:370
  88.8 9.7 %all-gather.2 = f32[4,1,128]{2,1,0:T(1,128)S(1)} all-gather(f32[1,1,128]{2,1,0:T(1,128)S(1)} %bitcast.30), channel_id=2, replica_groups=mesh['z'=8,'core'=2,'x'=4,'y'=8] {'x'}, dimensions={0}, use_global_device_ids=true | all-gather | bytes 2560 | tf_op jit(solution)/shard_map/all_gather | solution.py:370
  98.5 0.1 copy.16
  98.6 0.0 all-to-all-done.1
  98.6 0.0 copy-start.5
  98.6 0.6 broadcast_in_dim.56
  99.2 7.2 %all-to-all-start.2 = ((f32[8,1,128]{2,1,0:T(1,128)}), f32[8,1,128]{2,1,0:T(1,128)S(1)}, u32[]{:S(2)}, u32[]{:S(2)}) async-start(f32[8,1,128]{2,1,0:T(1,128)} %bitcast.10), calls=%async_computation.2 | async-start | bytes 8192 | tf_op jit(solution)/shard_map/all_to_all | solution.py:374
  106.5 0.0 copy-done.5
  106.5 2.6 %turn_back.1 = bf16[3,1,320,512]{3,2,1,0:T(8,128)(2,1)} custom-call(s32[1,1]{1,0:T(1,128)S(6)} %copy.17.count_ref, bf16[512,1024]{1,0:T(8,128)(2,1)} %bitcast.28), custom_call_target="tpu_custom_call" | custom-call | tf_op jit(solution)/shard_map/turn_back/pallas_call | solution.py:375
  109.1 3.6 %all-to-all-done.2 = f32[8,1,128]{2,1,0:T(1,128)S(1)} async-done(((f32[8,1,128]{2,1,0:T(1,128)}), f32[8,1,128]{2,1,0:T(1,128)S(1)}, u32[]{:S(2)}, u32[]{:S(2)}) %all-to-all-start.2) | async-done | bytes 4128 | tf_op jit(solution)/shard_map/all_to_all | solution.py:374
  112.6 0.6 slice_reduce_fusion
  113.9 0.6 divide_bitcast_fusion
  114.5 0.6 broadcast_divide_fusion
  (8 shorter events, 0.1 us)
Async XLA Ops:
  0.6 14.3 %copy-start = (bf16[128,16]{0,1:T(8,128)(2,1)S(1)}, bf16[128,16]{0,1:T(8,128)(2,1)}, u32[]{:S(2)}) copy-start(bf16[128,16]{0,1:T(8,128)(2,1)} %param.13) | copy-start | bytes 12292
  4.5 10.4 %copy-start.8 = (bf16[3,7,16]{2,1,0:T(8,128)(2,1)S(1)}, bf16[3,7,16]{2,1,0:T(8,128)(2,1)}, u32[]{:S(2)}) copy-start(bf16[3,7,16]{2,1,0:T(8,128)(2,1)} %param.12) | copy-start | bytes 2020
  4.5 10.4 %copy-start.6 = (bf16[128,256]{1,0:T(8,128)(2,1)S(1)}, bf16[128,256]{1,0:T(8,128)(2,1)}, u32[]{:S(2)}) copy-start(bf16[128,256]{1,0:T(8,128)(2,1)} %constant.27) | copy-start | bytes 196612
  4.5 10.6 %copy-start.7 = (bf16[128,256]{1,0:T(8,128)(2,1)S(1)}, bf16[128,256]{1,0:T(8,128)(2,1)}, u32[]{:S(2)}) copy-start(bf16[128,256]{1,0:T(8,128)(2,1)} %constant.28) | copy-start | bytes 196612
  4.5 45.3 %copy-start.1 = (bf16[256,768]{1,0:T(8,128)(2,1)S(1)}, bf16[256,768]{1,0:T(8,128)(2,1)}, u32[]{:S(2)}) copy-start(bf16[256,768]{1,0:T(8,128)(2,1)} %constant.22.clone.fs_ref) | copy-start | bytes 1179652
  4.5 45.3 %copy-start.2 = (bf16[256,768]{1,0:T(8,128)(2,1)S(1)}, bf16[256,768]{1,0:T(8,128)(2,1)}, u32[]{:S(2)}) copy-start(bf16[256,768]{1,0:T(8,128)(2,1)} %constant.23.clone.bs_ref) | copy-start | bytes 1179652
  4.5 45.3 %copy-start.3 = (bf16[768,128]{1,0:T(8,128)(2,1)S(1)}, bf16[768,128]{1,0:T(8,128)(2,1)}, u32[]{:S(2)}) copy-start(bf16[768,128]{1,0:T(8,128)(2,1)} %constant.21.clone.g_ref) | copy-start | bytes 589828
  4.5 45.3 %copy-start.4 = (bf16[256,256]{1,0:T(8,128)(2,1)S(1)}, bf16[256,256]{1,0:T(8,128)(2,1)}, u32[]{:S(2)}) copy-start(bf16[256,256]{1,0:T(8,128)(2,1)} %constant.20.clone.f_ref) | copy-start | bytes 393220
  4.5 44.2 %all-to-all-start = ((bf16[32,16,1280]{2,1,0:T(8,128)(2,1)}), bf16[32,16,1280]{2,1,0:T(8,128)(2,1)S(1)}, u32[]{:S(2)}, u32[]{:S(2)}) async-start(bf16[32,16,1280]{2,1,0:T(8,128)(2,1)} %bitcast.27), calls=%async_computation | async-start | bytes 2621440 | tf_op jit(solution)/shard_map/all_to_all | solution.py:319
  60.2 38.4 %all-to-all-start.1 = ((bf16[32,16,1024]{2,1,0:T(8,128)(2,1)}), bf16[32,16,1024]{2,1,0:T(8,128)(2,1)S(1)}, u32[]{:S(2)}, u32[]{:S(2)}) async-start(bf16[32,16,1024]{2,1,0:T(8,128)(2,1)} %get-tuple-element.10), calls=%async_computation.1 | async-start | bytes 2097152 | tf_op jit(solution)/shard_map/all_to_all | solution.py:368
  98.6 7.9 %copy-start.5 = (bf16[32,16,1024]{2,1,0:T(8,128)(2,1)}, bf16[32,16,1024]{2,1,0:T(8,128)(2,1)S(1)}, u32[]{:S(2)}) copy-start(bf16[32,16,1024]{2,1,0:T(8,128)(2,1)S(1)} %all-to-all-done.1) | copy-start | bytes 3145732
  99.2 13.4 %all-to-all-start.2 = ((f32[8,1,128]{2,1,0:T(1,128)}), f32[8,1,128]{2,1,0:T(1,128)S(1)}, u32[]{:S(2)}, u32[]{:S(2)}) async-start(f32[8,1,128]{2,1,0:T(1,128)} %bitcast.10), calls=%async_computation.2 | async-start | bytes 8192 | tf_op jit(solution)/shard_map/all_to_all | solution.py:374

commit v5 on v4

--- a/solution.py
+++ b/solution.py
@@ -305,6 +305,7 @@
     def local(streams, cotangent, counts, short_filters, long_filter):
         slots, channels = streams.shape[2:]
         own = channels // ctx
+        share = 256
         length = 8192
         nb = length // BLK
         total_params = float((LTAP + 3 * STAP) * channels * mesh.shape["dp"])
@@ -312,8 +313,13 @@
         turned = pl.pallas_call(
             turn_out_kernel,
             out_shape=jax.ShapeDtypeStruct((channels, 4 * slots), BF16),
-            in_specs=[smem, vmem, vmem],
-            out_specs=vmem,
+            grid=(channels // share,),
+            in_specs=[
+                smem,
+                pl.BlockSpec((3, 1, slots, share), lambda c: (0, 0, 0, c)),
+                pl.BlockSpec((1, slots, share), lambda c: (0, 0, c)),
+            ],
+            out_specs=pl.BlockSpec((share, 4 * slots), lambda c: (c, 0)),
             name="turn_out",
         )(counts, streams, cotangent)
         pieces = lax.all_to_all(
@@ -375,14 +381,15 @@
         stream_grads = pl.pallas_call(
             turn_back_kernel,
             out_shape=jax.ShapeDtypeStruct((3, 1, slots, channels), BF16),
-            in_specs=[smem, vmem],
-            out_specs=vmem,
+            grid=(channels // share,),
+            in_specs=[smem, pl.BlockSpec((share, 8 * BLK), lambda c: (c, 0))],
+            out_specs=pl.BlockSpec((3, 1, slots, share), lambda c: (0, 0, 0, c)),
             name="turn_back",
         )(counts, back.reshape(channels, 8 * BLK))
 
-        rms = jnp.sqrt(jnp.sum(shared[:, 0]) / total_params + 1e-06)
-        long_grad = (raw[0] / rms).T
-        short_grad = short_raw / rms
+        rms = jnp.sqrt(jnp.sum(shared, axis=0) / total_params + 1e-06)
+        long_grad = (raw[0] / rms[None]).T
+        short_grad = short_raw / rms[:own]
         return stream_grads, long_grad, short_grad
 
     return jax.shard_map(

time: 116 us -> 114 us (0.983)
  no operation moved by 1% of the time
where the time goes in v5:
time: 114 us
  waiting for transfers between devices  37.3 us (33%)
  blocking collectives  32.8 us (29%)
  starting transfers between devices  22.9 us (20%)
  Pallas kernels  15.8 us (14%)
  other arithmetic  2.22 us (2%)
  between operations  1.45 us (1%)
    all_to_all x1, waiting for transfers between devices, local(): lax.all_to_all(turned.reshape(ctx, own, 4 * slots), CTX, 0, 0, tiled=True)  33.6 us
    all_gather x2, blocking collectives, local(): lax.all_gather(shared, axis, axis=0, tiled=True)  32.8 us
    pallas_call x1, Pallas kernels, local(): pl.pallas_call(core_kernel, out_shape=(jax.ShapeDtypeStruct((ctx, own, 8...  10.4 us
    all_to_all x1, starting transfers between devices, local(): lax.all_to_all(turned.reshape(ctx, own, 4 * slots), CTX, 0, 0, tiled=True)  10.3 us
    all_to_all x1, starting transfers between devices, local(): shared = lax.all_to_all(shared, 'y', 0, 0, tiled=True)  7.23 us
    all_to_all x1, starting transfers between devices, local(): back = lax.all_to_all(grads, CTX, 0, 0, tiled=True)  5.41 us
    all_to_all x1, waiting for transfers between devices, local(): shared = lax.all_to_all(shared, 'y', 0, 0, tiled=True)  3.71 us
    pallas_call x1, Pallas kernels, local(): pl.pallas_call(turn_out_kernel, out_shape=jax.ShapeDtypeStruct((channels,...  2.95 us
  transfers between devices with their start and end apart: 3, of which 2 were waited for; matrix products, arithmetic and copies ran while one was open for 0% of the time, Pallas kernels for 2%

profile of v5, /device:TPU:8, one launch (start us, length us, event | category | flops | bytes accessed | tf_op | source)
XLA Modules:
  0.0 113.7 jit_solution(7908952573331201730)
XLA Ops:
  0.6 0.0 copy-start
  1.3 2.9 %turn_out.1 = bf16[512,1280]{1,0:T(8,128)(2,1)} custom-call(s32[1,1]{1,0:T(1,128)S(6)} %copy.17.count_ref, bf16[3,1,320,512]{3,2,1,0:T(8,128)(2,1)} %s_ref.1, bf16[1,320,512]{2,1,0:T(8,128)(2,1)} %d_ref.1), custom_call_target="tpu_custom_call" | custom-call | tf_op jit(solution)/shard_map/turn_out/pallas_call | solution.py:313
  4.3 0.0 copy-start.8
  4.3 0.0 copy-start.6
  4.3 0.0 copy-start.7
  4.3 0.0 copy-start.1
  4.3 0.0 copy-start.2
  4.3 0.0 copy-start.3
  4.3 0.0 copy-start.4
  4.3 10.3 %all-to-all-start = ((bf16[32,16,1280]{2,1,0:T(8,128)(2,1)}), bf16[32,16,1280]{2,1,0:T(8,128)(2,1)S(1)}, u32[]{:S(2)}, u32[]{:S(2)}) async-start(bf16[32,16,1280]{2,1,0:T(8,128)(2,1)} %bitcast.29), calls=%async_computation | async-start | bytes 2621440 | tf_op jit(solution)/shard_map/all_to_all | solution.py:325
  14.6 0.0 copy-done.8
  14.7 0.0 copy-done
  14.7 0.0 copy-done.6
  14.7 0.1 fusion.3
  14.8 0.0 copy-done.7
  14.8 0.1 fusion
  15.0 33.6 %all-to-all-done.r_ref = bf16[32,16,1280]{2,1,0:T(8,128)(2,1)S(1)} async-done(((bf16[32,16,1280]{2,1,0:T(8,128)(2,1)}), bf16[32,16,1280]{2,1,0:T(8,128)(2,1)S(1)}, u32[]{:S(2)}, u32[]{:S(2)}) %all-to-all-start) | async-done | bytes 1310752 | tf_op jit(solution)/shard_map/all_to_all | solution.py:325
  48.6 0.8 fusion.1
  49.3 0.1 select_reduce_fusion.off_ref
  49.4 0.1 broadcast_in_dim.56.w_ref
  49.6 0.0 copy-done.1
  49.6 0.0 copy-done.2
  49.6 0.0 copy-done.3
  49.6 0.0 copy-done.4
  49.6 10.4 %core.1 = (bf16[32,16,1024]{2,1,0:T(8,128)(2,1)}, f32[2,16,128]{2,1,0:T(8,128)S(1)}, f32[1,128]{1,0:T(1,128)S(1)}) custom-call(s32[32]{0:T(128)S(1)} %select_reduce_fusion.off_ref, bf16[32,16,1280]{2,1,0:T(8,128)(2,1)S(1)} %all-to-all-done.r_ref, f32[3,16,128]{2,1,0:T(8,128)S(1)} %pad_maximum_fusion.h_ref, f32[21,16,128]{2,1,0:T(8,128)S(1)} %broadcast_in_dim.56.w_ref, ...), custom_call_target="tpu_custom_call" | custom-call | tf_op jit(solution)/shard_map/core/pallas_call | solution.py:343
  60.0 5.4 %all-to-all-start.1 = ((bf16[32,16,1024]{2,1,0:T(8,128)(2,1)}), bf16[32,16,1024]{2,1,0:T(8,128)(2,1)S(1)}, u32[]{:S(2)}, u32[]{:S(2)}) async-start(bf16[32,16,1024]{2,1,0:T(8,128)(2,1)} %get-tuple-element.10), calls=%async_computation.1 | async-start | bytes 2097152 | tf_op jit(solution)/shard_map/all_to_all | solution.py:374
  65.4 23.2 %all-gather.1 = f32[16,1,128]{2,1,0:T(1,128)S(1)} all-gather(f32[1,1,128]{2,1,0:T(1,128)S(1)} %bitcast.28), channel_id=1, replica_groups=mesh['z'=8,'core'=2,'x'=4,'y'=8] {'z','core'}, dimensions={0}, use_global_device_ids=true | all-gather | bytes 8704 | tf_op jit(solution)/shard_map/all_gather | solution.py:376
  88.6 9.7 %all-gather.2 = f32[4,1,128]{2,1,0:T(1,128)S(1)} all-gather(f32[1,1,128]{2,1,0:T(1,128)S(1)} %bitcast.32), channel_id=2, replica_groups=mesh['z'=8,'core'=2,'x'=4,'y'=8] {'x'}, dimensions={0}, use_global_device_ids=true | all-gather | bytes 2560 | tf_op jit(solution)/shard_map/all_gather | solution.py:376
  98.3 0.1 copy.16
  98.4 0.0 all-to-all-done.1
  98.4 0.0 copy-start.5
  98.4 0.6 broadcast_in_dim.58
  99.0 7.2 %all-to-all-start.2 = ((f32[8,1,128]{2,1,0:T(1,128)}), f32[8,1,128]{2,1,0:T(1,128)S(1)}, u32[]{:S(2)}, u32[]{:S(2)}) async-start(f32[8,1,128]{2,1,0:T(1,128)} %bitcast.11), calls=%async_computation.2 | async-start | bytes 8192 | tf_op jit(solution)/shard_map/all_to_all | solution.py:380
  106.2 0.0 copy-done.5
  106.2 2.5 %turn_back.1 = bf16[3,1,320,512]{3,2,1,0:T(8,128)(2,1)} custom-call(s32[1,1]{1,0:T(1,128)S(6)} %copy.17.count_ref, bf16[512,1024]{1,0:T(8,128)(2,1)} %bitcast.30), custom_call_target="tpu_custom_call" | custom-call | tf_op jit(solution)/shard_map/turn_back/pallas_call | solution.py:381
  108.7 3.7 %all-to-all-done.2 = f32[8,1,128]{2,1,0:T(1,128)S(1)} async-done(((f32[8,1,128]{2,1,0:T(1,128)}), f32[8,1,128]{2,1,0:T(1,128)S(1)}, u32[]{:S(2)}, u32[]{:S(2)}) %all-to-all-start.2) | async-done | bytes 4128 | tf_op jit(solution)/shard_map/all_to_all | solution.py:380
  112.5 0.6 fusion.2
  113.1 0.6 broadcast_divide_fusion
  (10 shorter events, 0.1 us)
Async XLA Ops:
  0.6 14.0 %copy-start = (bf16[128,16]{0,1:T(8,128)(2,1)S(1)}, bf16[128,16]{0,1:T(8,128)(2,1)}, u32[]{:S(2)}) copy-start(bf16[128,16]{0,1:T(8,128)(2,1)} %param.13) | copy-start | bytes 12292
  4.3 10.4 %copy-start.8 = (bf16[3,7,16]{2,1,0:T(8,128)(2,1)S(1)}, bf16[3,7,16]{2,1,0:T(8,128)(2,1)}, u32[]{:S(2)}) copy-start(bf16[3,7,16]{2,1,0:T(8,128)(2,1)} %param.12) | copy-start | bytes 2020
  4.3 10.4 %copy-start.6 = (bf16[128,256]{1,0:T(8,128)(2,1)S(1)}, bf16[128,256]{1,0:T(8,128)(2,1)}, u32[]{:S(2)}) copy-start(bf16[128,256]{1,0:T(8,128)(2,1)} %constant.27) | copy-start | bytes 196612
  4.3 10.6 %copy-start.7 = (bf16[128,256]{1,0:T(8,128)(2,1)S(1)}, bf16[128,256]{1,0:T(8,128)(2,1)}, u32[]{:S(2)}) copy-start(bf16[128,256]{1,0:T(8,128)(2,1)} %constant.28) | copy-start | bytes 196612
  4.3 45.3 %copy-start.1 = (bf16[256,768]{1,0:T(8,128)(2,1)S(1)}, bf16[256,768]{1,0:T(8,128)(2,1)}, u32[]{:S(2)}) copy-start(bf16[256,768]{1,0:T(8,128)(2,1)} %constant.22.clone.fs_ref) | copy-start | bytes 1179652
  4.3 45.3 %copy-start.2 = (bf16[256,768]{1,0:T(8,128)(2,1)S(1)}, bf16[256,768]{1,0:T(8,128)(2,1)}, u32[]{:S(2)}) copy-start(bf16[256,768]{1,0:T(8,128)(2,1)} %constant.23.clone.bs_ref) | copy-start | bytes 1179652
  4.3 45.3 %copy-start.3 = (bf16[768,128]{1,0:T(8,128)(2,1)S(1)}, bf16[768,128]{1,0:T(8,128)(2,1)}, u32[]{:S(2)}) copy-start(bf16[768,128]{1,0:T(8,128)(2,1)} %constant.21.clone.g_ref) | copy-start | bytes 589828
  4.3 45.3 %copy-start.4 = (bf16[256,256]{1,0:T(8,128)(2,1)S(1)}, bf16[256,256]{1,0:T(8,128)(2,1)}, u32[]{:S(2)}) copy-start(bf16[256,256]{1,0:T(8,128)(2,1)} %constant.20.clone.f_ref) | copy-start | bytes 393220
  4.3 44.2 %all-to-all-start = ((bf16[32,16,1280]{2,1,0:T(8,128)(2,1)}), bf16[32,16,1280]{2,1,0:T(8,128)(2,1)S(1)}, u32[]{:S(2)}, u32[]{:S(2)}) async-start(bf16[32,16,1280]{2,1,0:T(8,128)(2,1)} %bitcast.29), calls=%async_computation | async-start | bytes 2621440 | tf_op jit(solution)/shard_map/all_to_all | solution.py:325
  60.0 38.4 %all-to-all-start.1 = ((bf16[32,16,1024]{2,1,0:T(8,128)(2,1)}), bf16[32,16,1024]{2,1,0:T(8,128)(2,1)S(1)}, u32[]{:S(2)}, u32[]{:S(2)}) async-start(bf16[32,16,1024]{2,1,0:T(8,128)(2,1)} %get-tuple-element.10), calls=%async_computation.1 | async-start | bytes 2097152 | tf_op jit(solution)/shard_map/all_to_all | solution.py:374
  98.4 7.9 %copy-start.5 = (bf16[32,16,1024]{2,1,0:T(8,128)(2,1)}, bf16[32,16,1024]{2,1,0:T(8,128)(2,1)S(1)}, u32[]{:S(2)}) copy-start(bf16[32,16,1024]{2,1,0:T(8,128)(2,1)S(1)} %all-to-all-done.1) | copy-start | bytes 3145732
  99.0 13.4 %all-to-all-start.2 = ((f32[8,1,128]{2,1,0:T(1,128)}), f32[8,1,128]{2,1,0:T(1,128)S(1)}, u32[]{:S(2)}, u32[]{:S(2)}) async-start(f32[8,1,128]{2,1,0:T(1,128)} %bitcast.11), calls=%async_computation.2 | async-start | bytes 8192 | tf_op jit(solution)/shard_map/all_to_all | solution.py:380

commit v6 on v5

--- a/solution.py
+++ b/solution.py
@@ -6,6 +6,7 @@
 from jax.experimental.pallas import tpu as pltpu
 from jax.sharding import Mesh
 from jax.sharding import PartitionSpec as P
+
 
 LTAP = 128
 STAP = 7
@@ -154,7 +155,7 @@
     lax.fori_loop(0, pieces, pack, 0, unroll=2)
 
     zero = jnp.zeros((chans, BLK), F32)
-    group = 32
+    group = 64
 
     def moved_blocks(first, second, table_ref):
         pairs = jnp.concatenate([first.reshape(-1, BLK), second.reshape(-1, BLK)], axis=1)
@@ -200,7 +201,7 @@
     sign = 1.0 - 2.0 * lax.bitwise_and(
         lax.broadcasted_iota(jnp.int32, (1, 1, FREQ), 2), 1
     ).astype(F32)
-    chunk = 32
+    chunk = 64
 
     def turn(re, im):
         rehi, relo = split2(re.reshape(-1, BLK))
@@ -276,7 +277,7 @@
         offset = off_ref[j]
         kept = []
         for part in range(3):
-            aligned, block, turned = place(offset, part)
+            _, block, turned = place(offset, part)
             back_by = lax.bitwise_and(BLK - turned, 127)
             early = lane < turned
             for n in range(3):

time: 114 us -> 114 us (level)
  no operation moved by 1% of the time
where the time goes in v6:
time: 114 us
  waiting for transfers between devices  37.3 us (33%)
  blocking collectives  32.8 us (29%)
  starting transfers between devices  22.9 us (20%)
  Pallas kernels  16 us (14%)
  other arithmetic  2.22 us (2%)
  between operations  1.45 us (1%)
    all_to_all x1, waiting for transfers between devices, local(): lax.all_to_all(turned.reshape(ctx, own, 4 * slots), CTX, 0, 0, tiled=True)  33.6 us
    all_gather x2, blocking collectives, local(): lax.all_gather(shared, axis, axis=0, tiled=True)  32.8 us
    pallas_call x1, Pallas kernels, local(): pl.pallas_call(core_kernel, out_shape=(jax.ShapeDtypeStruct((ctx, own, 8...  10.6 us
    all_to_all x1, starting transfers between devices, local(): lax.all_to_all(turned.reshape(ctx, own, 4 * slots), CTX, 0, 0, tiled=True)  10.3 us
    all_to_all x1, starting transfers between devices, local(): shared = lax.all_to_all(shared, 'y', 0, 0, tiled=True)  7.23 us
    all_to_all x1, starting transfers between devices, local(): back = lax.all_to_all(grads, CTX, 0, 0, tiled=True)  5.4 us
    all_to_all x1, waiting for transfers between devices, local(): shared = lax.all_to_all(shared, 'y', 0, 0, tiled=True)  3.72 us
    pallas_call x1, Pallas kernels, local(): pl.pallas_call(turn_out_kernel, out_shape=jax.ShapeDtypeStruct((channels,...  2.95 us
  transfers between devices with their start and end apart: 3, of which 2 were waited for; matrix products, arithmetic and copies ran while one was open for 0% of the time, Pallas kernels for 2%

profile of v6, /device:TPU:8, one launch (start us, length us, event | category | flops | bytes accessed | tf_op | source)
XLA Modules:
  0.0 113.9 jit_solution(16383189227483313567)
XLA Ops:
  0.6 0.0 copy-start
  1.3 2.9 %turn_out.1 = bf16[512,1280]{1,0:T(8,128)(2,1)} custom-call(s32[1,1]{1,0:T(1,128)S(6)} %copy.17.count_ref, bf16[3,1,320,512]{3,2,1,0:T(8,128)(2,1)} %s_ref.1, bf16[1,320,512]{2,1,0:T(8,128)(2,1)} %d_ref.1), custom_call_target="tpu_custom_call" | custom-call | tf_op jit(solution)/shard_map/turn_out/pallas_call | solution.py:314
  4.3 0.0 copy-start.8
  4.3 0.0 copy-start.6
  4.3 0.0 copy-start.7
  4.3 0.0 copy-start.1
  4.3 0.0 copy-start.2
  4.3 0.0 copy-start.3
  4.3 0.0 copy-start.4
  4.3 10.3 %all-to-all-start = ((bf16[32,16,1280]{2,1,0:T(8,128)(2,1)}), bf16[32,16,1280]{2,1,0:T(8,128)(2,1)S(1)}, u32[]{:S(2)}, u32[]{:S(2)}) async-start(bf16[32,16,1280]{2,1,0:T(8,128)(2,1)} %bitcast.29), calls=%async_computation | async-start | bytes 2621440 | tf_op jit(solution)/shard_map/all_to_all | solution.py:326
  14.6 0.0 copy-done.8
  14.7 0.0 copy-done
  14.7 0.0 copy-done.6
  14.7 0.1 fusion.3
  14.8 0.0 copy-done.7
  14.8 0.1 fusion
  15.0 33.6 %all-to-all-done.r_ref = bf16[32,16,1280]{2,1,0:T(8,128)(2,1)S(1)} async-done(((bf16[32,16,1280]{2,1,0:T(8,128)(2,1)}), bf16[32,16,1280]{2,1,0:T(8,128)(2,1)S(1)}, u32[]{:S(2)}, u32[]{:S(2)}) %all-to-all-start) | async-done | bytes 1310752 | tf_op jit(solution)/shard_map/all_to_all | solution.py:326
  48.6 0.8 fusion.1
  49.3 0.1 select_reduce_fusion.off_ref
  49.4 0.1 broadcast_in_dim.56.w_ref
  49.6 0.0 copy-done.1
  49.6 0.0 copy-done.2
  49.6 0.0 copy-done.3
  49.6 0.0 copy-done.4
  49.6 10.6 %core.1 = (bf16[32,16,1024]{2,1,0:T(8,128)(2,1)}, f32[2,16,128]{2,1,0:T(8,128)S(1)}, f32[1,128]{1,0:T(1,128)S(1)}) custom-call(s32[32]{0:T(128)S(1)} %select_reduce_fusion.off_ref, bf16[32,16,1280]{2,1,0:T(8,128)(2,1)S(1)} %all-to-all-done.r_ref, f32[3,16,128]{2,1,0:T(8,128)S(1)} %pad_maximum_fusion.h_ref, f32[21,16,128]{2,1,0:T(8,128)S(1)} %broadcast_in_dim.56.w_ref, ...), custom_call_target="tpu_custom_call" | custom-call | tf_op jit(solution)/shard_map/core/pallas_call | solution.py:344
  60.2 5.4 %all-to-all-start.1 = ((bf16[32,16,1024]{2,1,0:T(8,128)(2,1)}), bf16[32,16,1024]{2,1,0:T(8,128)(2,1)S(1)}, u32[]{:S(2)}, u32[]{:S(2)}) async-start(bf16[32,16,1024]{2,1,0:T(8,128)(2,1)} %get-tuple-element.10), calls=%async_computation.1 | async-start | bytes 2097152 | tf_op jit(solution)/shard_map/all_to_all | solution.py:375
  65.6 23.2 %all-gather.1 = f32[16,1,128]{2,1,0:T(1,128)S(1)} all-gather(f32[1,1,128]{2,1,0:T(1,128)S(1)} %bitcast.28), channel_id=1, replica_groups=mesh['z'=8,'core'=2,'x'=4,'y'=8] {'z','core'}, dimensions={0}, use_global_device_ids=true | all-gather | bytes 8704 | tf_op jit(solution)/shard_map/all_gather | solution.py:377
  88.8 9.7 %all-gather.2 = f32[4,1,128]{2,1,0:T(1,128)S(1)} all-gather(f32[1,1,128]{2,1,0:T(1,128)S(1)} %bitcast.32), channel_id=2, replica_groups=mesh['z'=8,'core'=2,'x'=4,'y'=8] {'x'}, dimensions={0}, use_global_device_ids=true | all-gather | bytes 2560 | tf_op jit(solution)/shard_map/all_gather | solution.py:377
  98.5 0.1 copy.16
  98.6 0.0 all-to-all-done.1
  98.6 0.0 copy-start.5
  98.6 0.6 broadcast_in_dim.58
  99.3 7.2 %all-to-all-start.2 = ((f32[8,1,128]{2,1,0:T(1,128)}), f32[8,1,128]{2,1,0:T(1,128)S(1)}, u32[]{:S(2)}, u32[]{:S(2)}) async-start(f32[8,1,128]{2,1,0:T(1,128)} %bitcast.11), calls=%async_computation.2 | async-start | bytes 8192 | tf_op jit(solution)/shard_map/all_to_all | solution.py:381
  106.5 0.0 copy-done.5
  106.5 2.5 %turn_back.1 = bf16[3,1,320,512]{3,2,1,0:T(8,128)(2,1)} custom-call(s32[1,1]{1,0:T(1,128)S(6)} %copy.17.count_ref, bf16[512,1024]{1,0:T(8,128)(2,1)} %bitcast.30), custom_call_target="tpu_custom_call" | custom-call | tf_op jit(solution)/shard_map/turn_back/pallas_call | solution.py:382
  108.9 3.7 %all-to-all-done.2 = f32[8,1,128]{2,1,0:T(1,128)S(1)} async-done(((f32[8,1,128]{2,1,0:T(1,128)}), f32[8,1,128]{2,1,0:T(1,128)S(1)}, u32[]{:S(2)}, u32[]{:S(2)}) %all-to-all-start.2) | async-done | bytes 4128 | tf_op jit(solution)/shard_map/all_to_all | solution.py:381
  112.7 0.6 fusion.2
  113.3 0.6 broadcast_divide_fusion
  (10 shorter events, 0.1 us)
Async XLA Ops:
  0.6 14.0 %copy-start = (bf16[128,16]{0,1:T(8,128)(2,1)S(1)}, bf16[128,16]{0,1:T(8,128)(2,1)}, u32[]{:S(2)}) copy-start(bf16[128,16]{0,1:T(8,128)(2,1)} %param.13) | copy-start | bytes 12292
  4.3 10.4 %copy-start.8 = (bf16[3,7,16]{2,1,0:T(8,128)(2,1)S(1)}, bf16[3,7,16]{2,1,0:T(8,128)(2,1)}, u32[]{:S(2)}) copy-start(bf16[3,7,16]{2,1,0:T(8,128)(2,1)} %param.12) | copy-start | bytes 2020
  4.3 10.4 %copy-start.6 = (bf16[128,256]{1,0:T(8,128)(2,1)S(1)}, bf16[128,256]{1,0:T(8,128)(2,1)}, u32[]{:S(2)}) copy-start(bf16[128,256]{1,0:T(8,128)(2,1)} %constant.27) | copy-start | bytes 196612
  4.3 10.6 %copy-start.7 = (bf16[128,256]{1,0:T(8,128)(2,1)S(1)}, bf16[128,256]{1,0:T(8,128)(2,1)}, u32[]{:S(2)}) copy-start(bf16[128,256]{1,0:T(8,128)(2,1)} %constant.28) | copy-start | bytes 196612
  4.3 45.3 %copy-start.1 = (bf16[256,768]{1,0:T(8,128)(2,1)S(1)}, bf16[256,768]{1,0:T(8,128)(2,1)}, u32[]{:S(2)}) copy-start(bf16[256,768]{1,0:T(8,128)(2,1)} %constant.22.clone.fs_ref) | copy-start | bytes 1179652
  4.3 45.3 %copy-start.2 = (bf16[256,768]{1,0:T(8,128)(2,1)S(1)}, bf16[256,768]{1,0:T(8,128)(2,1)}, u32[]{:S(2)}) copy-start(bf16[256,768]{1,0:T(8,128)(2,1)} %constant.23.clone.bs_ref) | copy-start | bytes 1179652
  4.3 45.3 %copy-start.3 = (bf16[768,128]{1,0:T(8,128)(2,1)S(1)}, bf16[768,128]{1,0:T(8,128)(2,1)}, u32[]{:S(2)}) copy-start(bf16[768,128]{1,0:T(8,128)(2,1)} %constant.21.clone.g_ref) | copy-start | bytes 589828
  4.3 45.3 %copy-start.4 = (bf16[256,256]{1,0:T(8,128)(2,1)S(1)}, bf16[256,256]{1,0:T(8,128)(2,1)}, u32[]{:S(2)}) copy-start(bf16[256,256]{1,0:T(8,128)(2,1)} %constant.20.clone.f_ref) | copy-start | bytes 393220
  4.3 44.2 %all-to-all-start = ((bf16[32,16,1280]{2,1,0:T(8,128)(2,1)}), bf16[32,16,1280]{2,1,0:T(8,128)(2,1)S(1)}, u32[]{:S(2)}, u32[]{:S(2)}) async-start(bf16[32,16,1280]{2,1,0:T(8,128)(2,1)} %bitcast.29), calls=%async_computation | async-start | bytes 2621440 | tf_op jit(solution)/shard_map/all_to_all | solution.py:326
  60.2 38.4 %all-to-all-start.1 = ((bf16[32,16,1024]{2,1,0:T(8,128)(2,1)}), bf16[32,16,1024]{2,1,0:T(8,128)(2,1)S(1)}, u32[]{:S(2)}, u32[]{:S(2)}) async-start(bf16[32,16,1024]{2,1,0:T(8,128)(2,1)} %get-tuple-element.10), calls=%async_computation.1 | async-start | bytes 2097152 | tf_op jit(solution)/shard_map/all_to_all | solution.py:375
  98.6 7.9 %copy-start.5 = (bf16[32,16,1024]{2,1,0:T(8,128)(2,1)}, bf16[32,16,1024]{2,1,0:T(8,128)(2,1)S(1)}, u32[]{:S(2)}) copy-start(bf16[32,16,1024]{2,1,0:T(8,128)(2,1)S(1)} %all-to-all-done.1) | copy-start | bytes 3145732
  99.3 13.4 %all-to-all-start.2 = ((f32[8,1,128]{2,1,0:T(1,128)}), f32[8,1,128]{2,1,0:T(1,128)S(1)}, u32[]{:S(2)}, u32[]{:S(2)}) async-start(f32[8,1,128]{2,1,0:T(1,128)} %bitcast.11), calls=%async_computation.2 | async-start | bytes 8192 | tf_op jit(solution)/shard_map/all_to_all | solution.py:381
